TPU v7x, 512 devices: a whole 4x8x8 slice. The times are simulated.
512 devices in a mesh: tile: 128 (over z, y, core), chan: 4 (over x).
Axes of the slice: x: 4, y: 8, z: 8, core: 2. Of those that a mesh axis runs over, the one named last changes fastest.
Arguments:
- features: bfloat16 [128, 192, 2304], P('tile', 'chan'), may hold values from -6 to 6
- land_mask: int32 [128, 2304], P('tile'), may hold values 0 or 1
- wet_slots: int32 [128], replicated, may hold values from 0 to 255, as said below
- device_of: int32 [128], replicated, may hold values from 0 to 127, as said below
- depth_weight: float32 [2, 192, 49], P(None, 'chan'), may hold values from -0.875 to 0.875
- depth_bias: float32 [2, 192], P(None, 'chan'), may hold values from -1.5 to 1.5
- norm_gain: float32 [2, 192], replicated, may hold values from 0.5 to 1.5
- norm_bias: float32 [2, 192], replicated, may hold values from -1.5 to 1.5
- up_weight: bfloat16 [2, 768, 192], replicated, may hold values from -0.4375 to 0.4375
- up_bias: float32 [2, 768], replicated, may hold values from -2.5 to 2.5
- down_weight: bfloat16 [2, 192, 768], replicated, may hold values from -0.21875 to 0.21875
- down_bias: float32 [2, 192], replicated, may hold values from -1.5 to 1.5
- layer_scale: float32 [2, 192], P(None, 'chan'), may hold values from 0.5 to 1.5
- pool_weight: float32 [192, 4], P('chan'), may hold values from -2.5 to 2.5
- spread_weight: float32 [192, 4], P('chan'), may hold values from -2.5 to 2.5
Outputs:
- merged: bfloat16 [128, 192, 2304], P('tile', 'chan')
Inputs may be any that keep to these rules, and one draw needn't show every extreme that they name: `wet_slots`: 128 distinct grid slots in increasing order, among them slots 0, 1 and the last slot. `device_of`: each device along tile holds exactly one wet tile; the tiles in slots 0 and 1 lie 128 / 2 devices apart, counted round. `land_mask`: 1 marks an ocean cell, 0 a land cell.
All inputs are finite; a program needn't handle non-finite values. No bound on the sum of `land_mask` on one device may be relied on, other than what follows from the above.
Results may differ from a plain program's by a relative error of at most 0.011.
Values may be sent and summed in bfloat16 or wider, within the bound.
A program may use at most 64 MiB of HBM per device.

v0:
```python
import functools

import jax
import jax.numpy as jnp
from jax import lax
from jax.experimental import pallas as pl
from jax.experimental.pallas import tpu as pltpu
from jax.sharding import PartitionSpec as P

TILE = 48
GRID_Y = 4
MESH = pl.DeviceIdType.MESH
BANDS = ((-1, -1), (-1, 0), (-1, 1), (0, -1), (0, 1), (1, -1), (1, 0), (1, 1))
norm_eps = 1e-06
VMEM_SPEC = pl.BlockSpec(memory_space=pltpu.VMEM)


def pick_table(wet_slots, device_of, grid_x, grid_y):
    tile_count = wet_slots.shape[0]
    devices = jnp.arange(tile_count, dtype=jnp.int32)
    slot = jnp.sum(jnp.where(device_of[None, :] == devices[:, None], wet_slots[None, :], 0), axis=1)
    column = slot % grid_x
    tile_row = slot // grid_x
    up = jnp.array([b[0] for b in BANDS], jnp.int32)[None, :]
    right = jnp.array([b[1] for b in BANDS], jnp.int32)[None, :]
    near_column = (column[:, None] + right) % grid_x
    near_row = tile_row[:, None] + up
    folded = near_row >= grid_y
    source_column = jnp.where(folded, grid_x - 1 - near_column, near_column)
    source_row = jnp.where(folded, grid_y - 1, near_row)
    source_slot = jnp.where(near_row < 0, -1, source_row * grid_x + source_column)
    strip = jnp.where(up == -1, 1, jnp.where(up == 1, jnp.where(folded, 1, 0), jnp.where(right == -1, 3, 2)))
    row_of_tile = device_of * 4 + 1
    found = jnp.sum(
        jnp.where(source_slot[:, :, None] == wet_slots[None, None, :], row_of_tile[None, None, :], 0), axis=2
    )
    table = jnp.where(found > 0, found - 1 + strip, tile_count * 4).astype(jnp.int32)
    return table, tile_row >= grid_y - 1


def halo_kernel(tiles, pieces, table_ref, strips_ref, got_ref, held, picked, send_a, recv_a, send_b, recv_b):
    me = lax.axis_index("tile")
    piece = (me * pieces + tiles - 1) // tiles
    holds = jnp.logical_and(piece < pieces, (piece * tiles) // pieces == me)
    holder = lambda p: (p * tiles) // pieces
    barrier = pltpu.get_barrier_semaphore()

    @pl.when(holds)
    def _():
        @pl.loop(1, tiles)
        def _(k):
            pl.semaphore_signal(barrier, inc=1, device_id={"tile": lax.rem(me + k, tiles)}, device_id_type=MESH)

        pl.semaphore_wait(barrier, tiles - 1)

    @pl.when(jnp.logical_not(holds))
    def _():
        @pl.loop(0, pieces)
        def _(p):
            pl.semaphore_signal(barrier, inc=1, device_id={"tile": holder(p)}, device_id_type=MESH)

        pl.semaphore_wait(barrier, pieces)

    @pl.loop(0, pieces)
    def _(p):
        target = holder(p)

        @pl.when(target != me)
        def _():
            pltpu.make_async_remote_copy(
                src_ref=strips_ref.at[p],
                dst_ref=held.at[pl.ds(me * 4, 4)],
                send_sem=send_a,
                recv_sem=recv_a,
                device_id={"tile": target},
                device_id_type=MESH,
            ).start()

    @pl.when(holds)
    def _():
        held[tiles * 4] = jnp.zeros(held.shape[1:], held.dtype)
        held[pl.ds(me * 4, 4)] = strips_ref[piece]
        everything = held.at[pl.ds(0, (tiles - 1) * 4)]
        pltpu.make_async_copy(everything, everything, recv_a).wait()

        @pl.loop(0, tiles)
        def _(k):
            target = lax.rem(me + k, tiles)
            for band in range(8):
                picked[target, band] = held[table_ref[target * 8 + band]]

            @pl.when(k > 0)
            def _():
                pltpu.make_async_remote_copy(
                    src_ref=picked.at[target],
                    dst_ref=got_ref.at[piece],
                    send_sem=send_b,
                    recv_sem=recv_b,
                    device_id={"tile": target},
                    device_id_type=MESH,
                ).start()

        got_ref[piece] = picked[me]
        others = strips_ref.at[pl.ds(0, pieces - 1)]
        pltpu.make_async_copy(others, others, send_a).wait()
        arrived = got_ref.at[pl.ds(0, pieces - 1)]
        pltpu.make_async_copy(arrived, arrived, recv_b).wait()
        left = picked.at[pl.ds(0, tiles - 1)]
        pltpu.make_async_copy(left, left, send_b).wait()

    @pl.when(jnp.logical_not(holds))
    def _():
        pltpu.make_async_copy(strips_ref, strips_ref, send_a).wait()
        pltpu.make_async_copy(got_ref, got_ref, recv_b).wait()


def exchange(strips, table, call_id):
    tiles = table.shape[0]
    length = strips.shape[1]
    pieces = -(-length // 256)
    padded = jnp.pad(strips, ((0, 0), (0, pieces * 256 - length)))
    cut = padded.reshape(4, pieces, 2, 128).transpose(1, 0, 2, 3)
    got = pl.pallas_call(
        functools.partial(halo_kernel, tiles, pieces),
        out_shape=jax.ShapeDtypeStruct((pieces, 8, 2, 128), jnp.bfloat16),
        in_specs=[pl.BlockSpec(memory_space=pltpu.SMEM), VMEM_SPEC],
        out_specs=VMEM_SPEC,
        scratch_shapes=[
            pltpu.VMEM((tiles * 4 + 1, 2, 128), jnp.bfloat16),
            pltpu.VMEM((tiles, 8, 2, 128), jnp.bfloat16),
            pltpu.SemaphoreType.DMA,
            pltpu.SemaphoreType.DMA,
            pltpu.SemaphoreType.DMA,
            pltpu.SemaphoreType.DMA,
        ],
        compiler_params=pltpu.CompilerParams(collective_id=call_id, has_side_effects=True),
        name=f"halo_{call_id}",
    )(table.reshape(-1), cut)
    return got.transpose(1, 0, 2, 3).reshape(8, pieces * 256)[:, :length]


def mix_kernel(
    ways, conv_ref, gain_ref, bias_ref, up_ref, upb_ref, down_ref, downb_ref, out_ref, every, acc, branch, sa, ra, sb, rb
):
    me = lax.axis_index("chan")
    barrier = pltpu.get_barrier_semaphore()
    for k in range(1, ways):
        pl.semaphore_signal(barrier, inc=1, device_id={"chan": lax.rem(me + k, ways)}, device_id_type=MESH)
    pl.semaphore_wait(barrier, ways - 1)
    copies = []
    for k in range(1, ways):
        peer = lax.rem(me + k, ways)
        copy = pltpu.make_async_remote_copy(
            src_ref=conv_ref.at[peer],
            dst_ref=every.at[me],
            send_sem=sa.at[k],
            recv_sem=ra.at[k],
            device_id={"chan": peer},
            device_id_type=MESH,
        )
        copy.start()
        copies.append(copy)
    every[me] = conv_ref[me]
    for copy in copies:
        copy.wait()
    values = every[...].astype(jnp.float32)
    group, rows, cells = values.shape
    count = group * rows
    mean = jnp.sum(jnp.sum(values, axis=0), axis=0, keepdims=True) * (1.0 / count)
    centred = values - mean[None]
    spread = jnp.sum(jnp.sum(centred * centred, axis=0), axis=0, keepdims=True) * (1.0 / count)
    scaled = (centred * lax.rsqrt(spread + norm_eps)[None]).reshape(count, cells)
    normed = (scaled * gain_ref[...] + bias_ref[...]).astype(jnp.bfloat16)
    acc[...] = jnp.broadcast_to(downb_ref[...], acc.shape)
    hidden_size = up_ref.shape[0]
    step = 256

    @pl.loop(0, hidden_size // step)
    def _(i):
        at = pl.multiple_of(i * step, step)
        hidden = jnp.dot(up_ref[pl.ds(at, step), :], normed, preferred_element_type=jnp.float32)
        hidden = hidden + upb_ref[pl.ds(at, step), :]
        hidden = 0.5 * hidden * (1.0 + lax.erf(hidden * (0.5**0.5)))
        acc[...] += jnp.dot(
            down_ref[:, pl.ds(at, step)], hidden.astype(jnp.bfloat16), preferred_element_type=jnp.float32
        )

    branch[...] = acc[...].astype(jnp.bfloat16).reshape(branch.shape)
    copies = []
    for k in range(1, ways):
        peer = lax.rem(me + k, ways)
        copy = pltpu.make_async_remote_copy(
            src_ref=branch.at[peer],
            dst_ref=out_ref.at[me],
            send_sem=sb.at[k],
            recv_sem=rb.at[k],
            device_id={"chan": peer},
            device_id_type=MESH,
        )
        copy.start()
        copies.append(copy)
    out_ref[me] = branch[me]
    for copy in copies:
        copy.wait()


def mix(conv, params, ways, call_id):
    rows, cells = conv.shape
    part = cells // ways
    cut = conv.reshape(rows, ways, part).transpose(1, 0, 2)
    shape = (ways, rows, part)
    out = pl.pallas_call(
        functools.partial(mix_kernel, ways),
        out_shape=jax.ShapeDtypeStruct(shape, jnp.bfloat16),
        in_specs=[VMEM_SPEC] * 7,
        out_specs=VMEM_SPEC,
        scratch_shapes=[
            pltpu.VMEM(shape, jnp.bfloat16),
            pltpu.VMEM((ways * rows, part), jnp.float32),
            pltpu.VMEM(shape, jnp.bfloat16),
        ]
        + [pltpu.SemaphoreType.DMA((ways,))] * 4,
        compiler_params=pltpu.CompilerParams(collective_id=call_id, has_side_effects=True),
        name=f"mix_{call_id}",
    )(cut, params[2][:, None], params[3][:, None], params[4], params[5][:, None], params[6], params[7][:, None])
    return out.transpose(1, 0, 2).reshape(rows, cells)


def edge_strips(tile_grid):
    tile_side = tile_grid.shape[-1]
    first_rows = tile_grid[..., :3, :]
    last_rows = tile_grid[..., tile_side - 3 :, :]
    first_cols = jnp.swapaxes(tile_grid[..., :, :3], -1, -2)
    last_cols = jnp.swapaxes(tile_grid[..., :, tile_side - 3 :], -1, -2)
    return jnp.stack([first_rows, last_rows, first_cols, last_cols], axis=-4)


def padded_tile(own_tile, raw_strips, flip):
    tile_side = own_tile.shape[-1]
    band_list = []
    for band_index, (up_by, right_by) in enumerate(BANDS):
        piece_in = raw_strips[band_index]
        if up_by != 0:
            if up_by == 1:
                piece_in = jnp.where(flip, piece_in[:, ::-1, ::-1], piece_in)
            if right_by == -1:
                piece_in = piece_in[:, :, tile_side - 3 :]
            elif right_by == 1:
                piece_in = piece_in[:, :, :3]
        else:
            piece_in = jnp.swapaxes(piece_in, 1, 2)
        band_list.append(piece_in)
    lower_rows = jnp.concatenate([band_list[0], band_list[1], band_list[2]], axis=2)
    middle_rows = jnp.concatenate([band_list[3], own_tile, band_list[4]], axis=2)
    upper_rows = jnp.concatenate([band_list[5], band_list[6], band_list[7]], axis=2)
    return jnp.concatenate([lower_rows, middle_rows, upper_rows], axis=1)


def depthwise(padded, weights, bias_row):
    chan_rows = padded.shape[0]
    padded_side = padded.shape[1]
    tile_side = padded_side - 6
    flat_cells = padded.astype(jnp.float32).reshape(chan_rows, padded_side * padded_side)
    flat_cells = jnp.pad(flat_cells, ((0, 0), (0, 6)))
    span_cells = tile_side * padded_side
    running = jnp.zeros((chan_rows, span_cells), jnp.float32)
    for row_step in range(7):
        for col_step in range(7):
            offset = row_step * padded_side + col_step
            running = (
                running
                + weights[:, row_step * 7 + col_step][:, None] * flat_cells[:, offset : offset + span_cells]
            )
    conv_out = running.reshape(chan_rows, tile_side, padded_side)[:, :, :tile_side] + bias_row[:, None, None]
    return conv_out.astype(jnp.bfloat16)


def pool_cells(tile_grid, weights):
    values = tile_grid.astype(jnp.float32)
    running = weights[:, 0][:, None, None] * values[:, 0::2, 0::2]
    running = running + weights[:, 1][:, None, None] * values[:, 0::2, 1::2]
    running = running + weights[:, 2][:, None, None] * values[:, 1::2, 0::2]
    running = running + weights[:, 3][:, None, None] * values[:, 1::2, 1::2]
    return running.astype(jnp.bfloat16)


def coarse_mask(mask_grid):
    half_side = mask_grid.shape[0] // 2
    return jnp.max(mask_grid.reshape(half_side, 2, half_side, 2), axis=(1, 3))


def join_levels(fine_flat, coarse_flat, weights, cell_mask, tile_side):
    chan_rows = fine_flat.shape[0]
    half_side = tile_side // 2
    coarse_vals = coarse_flat.astype(jnp.float32).reshape(chan_rows, half_side, half_side)
    spread = weights.reshape(chan_rows, 2, 2)
    expanded = coarse_vals[:, :, None, :, None] * spread[:, None, :, None, :]
    expanded = expanded.reshape(chan_rows, tile_side * tile_side)
    return (cell_mask[None, :] * (fine_flat.astype(jnp.float32) + expanded)).astype(jnp.bfloat16)


def level_body(flat_tile, tile_side, params, cell_mask, table, flip, ways, ids):
    chan_rows = flat_tile.shape[0]
    cell_count = tile_side * tile_side
    tile_grid = flat_tile.reshape(chan_rows, tile_side, tile_side)
    strips = edge_strips(tile_grid).reshape(4, chan_rows * 3 * tile_side)
    got = exchange(strips, table, ids[0])
    raw_strips = [got[band].reshape(chan_rows, 3, tile_side) for band in range(8)]
    padded = padded_tile(tile_grid, raw_strips, flip)
    conv_out = depthwise(padded, params[0], params[1]).reshape(chan_rows, cell_count)
    branch = mix(conv_out, params, ways, ids[1]).astype(jnp.float32)
    scale_row = params[8]
    return (
        cell_mask[None, :] * (flat_tile.astype(jnp.float32) + scale_row[:, None] * branch)
    ).astype(jnp.bfloat16)


def per_device(
    ways,
    features,
    land_mask,
    wet_slots,
    device_of,
    depth_weight,
    depth_bias,
    norm_gain,
    norm_bias,
    up_weight,
    up_bias,
    down_weight,
    down_bias,
    layer_scale,
    pool_weight,
    spread_weight,
):
    tile_count = wet_slots.shape[0]
    table, folded = pick_table(wet_slots, device_of, 2 * tile_count // GRID_Y, GRID_Y)
    flip = lax.dynamic_index_in_dim(folded, lax.axis_index("tile"), 0, keepdims=False)
    stacks = (
        depth_weight,
        depth_bias,
        norm_gain,
        norm_bias,
        up_weight,
        up_bias,
        down_weight,
        down_bias,
        layer_scale,
    )
    fine_params = tuple((array[0] for array in stacks))
    coarse_params = tuple((array[1] for array in stacks))
    fine_mask = land_mask[0].astype(jnp.float32)
    fine_out = level_body(features[0], TILE, fine_params, fine_mask, table, flip, ways, (0, 1))
    chan_rows = fine_out.shape[0]
    half_side = TILE // 2
    pooled = pool_cells(fine_out.reshape(chan_rows, TILE, TILE), pool_weight).reshape(
        chan_rows, half_side * half_side
    )
    small_mask = (
        coarse_mask(land_mask[0].reshape(TILE, TILE)).reshape(half_side * half_side).astype(jnp.float32)
    )
    coarse = level_body(pooled, half_side, coarse_params, small_mask, table, flip, ways, (2, 3))
    merged = join_levels(fine_out, coarse, spread_weight, fine_mask, TILE)
    return merged[None]


def solution(mesh):
    placed = (
        P("tile", "chan", None),
        P("tile", None),
        P(),
        P(),
        P(None, "chan", None),
        P(None, "chan"),
        P(),
        P(),
        P(),
        P(),
        P(),
        P(),
        P(None, "chan"),
        P("chan", None),
        P("chan", None),
    )
    return jax.shard_map(
        functools.partial(per_device, mesh.shape["chan"]),
        mesh=mesh,
        in_specs=placed,
        out_specs=P("tile", "chan", None),
        check_vma=False,
    )
```

profile of v0, /device:TPU:1, one launch (start us, length us, event | category | flops | bytes accessed | tf_op | source)
XLA Modules:
  0.0 144.5 jit_solution(2898201284809762698)
XLA Ops:
  0.1 1.3 copy.95
  3.4 2.4 %select_reduce_fusion = s32[128,8]{1,0:T(8,128)S(1)} fusion(s32[128]{0:T(128)S(1)} %multiply_add_fusion, s32[128]{0:T(128)S(1)} %copy-done.15, s32[128,8]{1,0:T(8,128)S(1)} %fusion.110), kind=kLoop, calls=%fused_computation.6 | loop fusion | flops 392192 | bytes 9216 | tf_op jit(solution)/shard_map/reduce_sum | solution.py:34
  6.6 33.5 %halo_0.1 = bf16[27,8,2,128]{3,2,1,0:T(2,128)(2,1)} custom-call(s32[1024]{0:T(1024)} %reshape.330.table_ref, bf16[27,4,2,128]{3,2,1,0:T(2,128)(2,1)} %maximum_bitcast_fusion.strips_ref), custom_call_target="tpu_custom_call" | custom-call | tf_op jit(solution)/shard_map/halo_0/pallas_call | solution.py:123
  40.1 0.9 fusion.123
  45.9 1.3 reshape.331
  47.1 1.8 %copy.152 = f32[48,2916]{1,0:T(8,128)S(1)} copy(f32[48,2916]{0,1:T(8,128)} %reshape.331) | data formatting | bytes 1119744 | tf_op jit(solution)/shard_map/convert_element_type | solution.py:263
  50.6 7.7 %fusion.8 = f32[48,2592]{1,0:T(8,128)S(1)} fusion(f32[48,2916]{1,0:T(8,128)S(1)} %copy.152, f32[48]{0:T(128)S(1)} %get-tuple-element.63, f32[48]{0:T(128)S(1)} %get-tuple-element.64, f32[48]{0:T(128)S(1)} %get-tuple-element.65, f32[48]{0:T(128)S(1)} %get-tuple-element.66, f32[48]{0:T(128)S(1)} %get-tuple-element.67, f32[48]{0:T(128)S(1)} %get-tuple-element.68, ...), kind=kLoop, calls=%fused_computation.14 | loop fusion | flops 12068352 | bytes 23280128 | tf_op jit(solution)/shard_map/add | solution.py:271
  58.3 0.9 reshape.317
  61.4 0.9 copy.158
  62.3 0.9 slice_bitcast_fusion
  63.2 0.9 copy.120.upb_ref
  64.1 0.8 copy.118.gain_ref
  66.4 17.6 %mix_1.1 = bf16[4,48,576]{2,1,0:T(8,128)(2,1)} custom-call(bf16[4,48,576]{2,1,0:T(8,128)(2,1)} %bitcast.114, f32[192,1]{1,0:T(8,128)} %copy.118.gain_ref, f32[192,1]{1,0:T(8,128)} %copy.119.bias_ref, bf16[768,192]{1,0:T(8,128)(2,1)} %bitcast.111, f32[768,1]{1,0:T(8,128)} %copy.120.upb_ref, bf16[192,768]{1,0:T(8,128)(2,1)} %get-tuple-element.114.down_ref, ...), custom_call_target="tpu_custom_call" | custom-call | tf_op jit(solution)/shard_map/mix_1/pallas_call | solution.py:212
  84.0 1.0 convert_bitcast_fusion
  86.5 1.1 slice.1003
  87.6 1.1 slice.1005
  91.1 23.5 %halo_2.1 = bf16[14,8,2,128]{3,2,1,0:T(2,128)(2,1)} custom-call(s32[1024]{0:T(1024)} %reshape.330.table_ref, bf16[14,4,2,128]{3,2,1,0:T(2,128)(2,1)} %bitcast.124), custom_call_target="tpu_custom_call" | custom-call | tf_op jit(solution)/shard_map/halo_2/pallas_call | solution.py:123
  114.6 0.8 copy.130
  120.7 2.8 %fusion.57 = f32[48,720]{0,1:T(8,128)S(1)} fusion(f32[48,900]{0,1:T(8,128)S(1)} %reshape.326, f32[48]{0:T(128)S(1)} %get-tuple-element.14, f32[48]{0:T(128)S(1)} %get-tuple-element.15, f32[48]{0:T(128)S(1)} %get-tuple-element.16, f32[48]{0:T(128)S(1)} %get-tuple-element.17, f32[48]{0:T(128)S(1)} %get-tuple-element.18, f32[48]{0:T(128)S(1)} %get-tuple-element.19, ...), kind=kLoop, calls=%fused_computation.110 | loop fusion | flops 3352320 | bytes 16477696 | tf_op jit(solution)/shard_map/add | solution.py:271
  124.5 0.9 copy.161
  125.4 0.9 copy.148.upb_ref
  128.6 11.2 %mix_3.1 = bf16[4,48,144]{2,1,0:T(8,128)(2,1)} custom-call(bf16[4,48,144]{2,1,0:T(8,128)(2,1)} %bitcast.118, f32[192,1]{1,0:T(8,128)} %copy.146.gain_ref, f32[192,1]{1,0:T(8,128)} %copy.147.bias_ref, bf16[768,192]{1,0:T(8,128)(2,1)} %bitcast.112, f32[768,1]{1,0:T(8,128)} %copy.148.upb_ref, bf16[192,768]{1,0:T(8,128)(2,1)} %get-tuple-element.113.down_ref, ...), custom_call_target="tpu_custom_call" | custom-call | tf_op jit(solution)/shard_map/mix_3/pallas_call | solution.py:212
  139.9 0.9 convert_bitcast_fusion.1
  143.7 0.8 multiply_convert_fusion.1
  (166 shorter events, 27.8 us)
Async XLA Ops:
  0.0 3.3 %copy-start.8 = (s32[8]{0:T(128)S(1)}, s32[8]{0:T(128)}, u32[]{:S(2)}) copy-start(s32[8]{0:T(128)} %constant.78.clone) | copy-start | bytes 100
  0.0 3.3 %copy-start.19 = (s32[8]{0:T(128)S(1)}, s32[8]{0:T(128)}, u32[]{:S(2)}) copy-start(s32[8]{0:T(128)} %constant.79.clone) | copy-start | bytes 100
  0.0 5.8 %copy-start.16 = (pred[8]{0:T(512)(128)(4,1)S(1)}, pred[8]{0:T(512)(128)(4,1)}, u32[]{:S(2)}) copy-start(pred[8]{0:T(512)(128)(4,1)} %constant.88) | copy-start | bytes 28
  0.0 5.8 %copy-start.17 = (pred[8]{0:T(512)(128)(4,1)S(1)}, pred[8]{0:T(512)(128)(4,1)}, u32[]{:S(2)}) copy-start(pred[8]{0:T(512)(128)(4,1)} %constant.89) | copy-start | bytes 28
  0.0 5.8 %copy-start.18 = (s32[8]{0:T(128)S(1)}, s32[8]{0:T(128)}, u32[]{:S(2)}) copy-start(s32[8]{0:T(128)} %constant.91) | copy-start | bytes 100
  0.0 3.1 %copy-start.15 = (s32[128]{0:T(128)S(1)}, s32[128]{0:T(128)}, u32[]{:S(2)}) copy-start(s32[128]{0:T(128)} %param.19) | copy-start | bytes 1540
  0.0 3.1 %copy-start.20 = (s32[128]{0:T(128)S(1)}, s32[128]{0:T(128)}, u32[]{:S(2)}) copy-start(s32[128]{0:T(128)} %param.20) | copy-start | bytes 1540
  47.1 1.8 %copy-start.4 = (f32[2,48,49]{2,1,0:T(8,128)S(1)}, f32[2,48,49]{2,1,0:T(8,128)}, u32[]{:S(2)}) copy-start(f32[2,48,49]{2,1,0:T(8,128)} %param.21) | copy-start | bytes 56452
  58.3 0.9 copy-start.13
  59.2 1.4 copy-start.2
  59.4 2.9 %copy-start.3 = (bf16[2,192,768]{2,1,0:T(8,128)(2,1)S(1)}, bf16[2,192,768]{2,1,0:T(8,128)(2,1)}, u32[]{:S(2)}) copy-start(bf16[2,192,768]{2,1,0:T(8,128)(2,1)} %param.27) | copy-start | bytes 1769476
  60.6 2.6 %copy-start.6 = (f32[2,768]{1,0:T(2,128)S(1)}, f32[2,768]{1,0:T(2,128)}, u32[]{:S(2)}) copy-start(f32[2,768]{1,0:T(2,128)} %param.26) | copy-start | bytes 18436
  60.6 3.5 %copy-start.9 = (f32[2,192]{1,0:T(2,128)S(1)}, f32[2,192]{1,0:T(2,128)}, u32[]{:S(2)}) copy-start(f32[2,192]{1,0:T(2,128)} %param.23) | copy-start | bytes 4612
  60.6 4.3 %copy-start.10 = (f32[2,192]{1,0:T(2,128)S(1)}, f32[2,192]{1,0:T(2,128)}, u32[]{:S(2)}) copy-start(f32[2,192]{1,0:T(2,128)} %param.24) | copy-start | bytes 4612
  61.4 4.3 %copy-start.11 = (f32[2,192]{1,0:T(2,128)S(1)}, f32[2,192]{1,0:T(2,128)}, u32[]{:S(2)}) copy-start(f32[2,192]{1,0:T(2,128)} %param.28) | copy-start | bytes 4612
  84.0 1.4 copy-start.14
  84.0 1.4 copy-start.5
  86.0 3.2 %copy-start.12 = (f32[48,4]{0,1:T(4,128)S(1)}, f32[48,4]{0,1:T(4,128)}, u32[]{:S(2)}) copy-start(f32[48,4]{0,1:T(4,128)} %param.30) | copy-start | bytes 2308
  123.5 1.0 copy-start
  139.9 2.3 %copy-start.7 = (f32[48,4]{0,1:T(4,128)S(1)}, f32[48,4]{0,1:T(4,128)}, u32[]{:S(2)}) copy-start(f32[48,4]{0,1:T(4,128)} %param.31) | copy-start | bytes 2308
  142.7 0.9 copy-start.1
where the time goes:
time: 146 us; the launch traced here: 145 us
  Pallas kernels  85.8 us (59%)
  local copies, waits for them, and re-layouts  35.7 us (24%)
  other arithmetic  22.2 us (15%)
    pallas_call x2, Pallas kernels, exchange(): pl.pallas_call(functools.partial(halo_kernel, tiles, pieces), out_shape=j...  57 us
    pallas_call x2, Pallas kernels, mix(): pl.pallas_call(functools.partial(mix_kernel, ways), out_shape=jax.ShapeDt...  28.8 us
    add x2, other arithmetic, depthwise(): running + weights[:, row_step * 7 + col_step][:, None] * flat_cells[:, of...  10.5 us
    unnamed x49, local copies, waits for them, and re-layouts  3.84 us
    slice x6, local copies, waits for them, and re-layouts, depthwise(): weights[:, row_step * 7 + col_step][:, None]  3.17 us
    select_n x5, other arithmetic, padded_tile(): piece_in = jnp.where(flip, piece_in[:, ::-1, ::-1], piece_in)  3.16 us
    convert_element_type x3, local copies, waits for them, and re-layouts, depthwise(): padded.astype(jnp.float32).reshape(chan_rows, padded_side * padded_side)  3.12 us
    another operation x28, local copies, waits for them, and re-layouts, level_body(): got[band].reshape(chan_rows, 3, tile_side)  3.07 us

commit v1 on v0

v1 whole, which is shorter than its diff:
```python
import functools

import jax
import jax.numpy as jnp
from jax import lax
from jax.experimental import pallas as pl
from jax.experimental.pallas import tpu as pltpu
from jax.sharding import PartitionSpec as P

TILE = 48
GRID_Y = 4
MESH = pl.DeviceIdType.MESH
norm_eps = 1e-06
VMEM_SPEC = pl.BlockSpec(memory_space=pltpu.VMEM)
SMEM_SPEC = pl.BlockSpec(memory_space=pltpu.SMEM)
LANES = 128
F32 = jnp.float32
BF16 = jnp.bfloat16


class Level:
    def __init__(self, side, parts, slots):
        self.side = side
        self.parts = parts
        self.pitch = LANES // parts
        self.rows = side // parts
        self.slots = slots
        self.edge_units = -(-3 // parts)
        self.side_units = -(-self.rows // slots)
        self.units = 2 * self.edge_units + self.side_units


FINE = Level(TILE, 2, 8)
COARSE = Level(TILE // 2, 4, 3)
MIX_ROWS = (6, 2)


def roll(x, shift):
    shift %= LANES
    return x if shift == 0 else pltpu.roll(x, shift, x.ndim - 1)


def source_table(wet_slots, device_of, grid_x, grid_y):
    tile_count = wet_slots.shape[0]
    devices = jnp.arange(tile_count, dtype=jnp.int32)
    slot = jnp.sum(jnp.where(device_of[None, :] == devices[:, None], wet_slots[None, :], 0), axis=1)
    column = (slot % grid_x)[:, None]
    tile_row = (slot // grid_x)[:, None]
    band = lax.broadcasted_iota(jnp.int32, (1, 8), 1)
    up = jnp.where(band < 3, -1, jnp.where(band < 5, 0, 1))
    right = jnp.where(band < 3, band - 1, jnp.where(band < 5, 2 * band - 7, band - 6))
    near_row = tile_row + up
    folded = near_row >= grid_y
    right = jnp.where(folded, -right, right)
    near_column = (column + right) % grid_x
    source_column = jnp.where(folded, grid_x - 1 - near_column, near_column)
    source_row = jnp.where(folded, grid_y - 1, near_row)
    source_slot = jnp.where(near_row < 0, -1, source_row * grid_x + source_column)
    found = jnp.sum(
        jnp.where(source_slot[:, :, None] == wet_slots[None, None, :], device_of[None, None, :] + 1, 0), axis=2
    )
    table = jnp.where(found > 0, found - 1, tile_count)
    at_fold = (tile_row >= grid_y - 1).astype(jnp.int32)
    return jnp.concatenate([table, at_fold], axis=1)


def lane_ids(shape=(1, LANES)):
    return lax.broadcasted_iota(jnp.int32, shape, len(shape) - 1)


def cut_units(level, grid, units, outgoing):
    lane = lane_ids()
    q = lax.rem(lane, level.pitch)
    part = lane // level.pitch
    side, rows, pitch = level.side, level.rows, level.pitch

    def periodic(j):
        own = grid[j]
        own = jnp.where(q < 3, roll(own, -side), own)
        return jnp.where(q >= side + 3, roll(own, side), own)

    for edge in range(2):
        at = 0 if edge == 0 else level.parts - 1
        for unit in range(level.edge_units):
            value = None
            for k in range(3):
                if k // level.parts != unit:
                    continue
                row = roll(periodic((3 if edge == 0 else rows) + k), (k % level.parts - at) * pitch)
                value = row if value is None else jnp.where(part == k % level.parts, row, value)
            units[edge * level.edge_units + unit] = value.astype(BF16)
    for unit in range(level.side_units):
        value = None
        for slot in range(level.slots):
            j = unit * level.slots + slot
            if j >= rows:
                continue
            own = grid[3 + j]
            both = jnp.where(q < 6 * slot + 3, roll(own, 6 * slot - 3), roll(own, 6 * slot + 3 - side))
            value = both if value is None else jnp.where(q < 6 * slot, value, both)
        units[2 * level.edge_units + unit] = value.astype(BF16)
    pairs = outgoing.shape[0]
    for unit in range(level.units):
        for p in range(pairs):
            outgoing[p, unit] = units[unit, 2 * p : 2 * p + 2, :]


def route(level, tiles, table_ref, outgoing, held, picked, got, send_a, recv_a, send_b, recv_b):
    me = lax.axis_index("tile")
    pieces = outgoing.shape[0]
    piece = (me * pieces + tiles - 1) // tiles
    holds = jnp.logical_and(piece < pieces, (piece * tiles) // pieces == me)
    units, edge = level.units, level.edge_units

    @pl.loop(0, pieces)
    def _(p):
        target = (p * tiles) // pieces

        @pl.when(target != me)
        def _():
            pltpu.make_async_remote_copy(
                src_ref=outgoing.at[p],
                dst_ref=held.at[pl.ds(me * units, units)],
                send_sem=send_a,
                recv_sem=recv_a,
                device_id={"tile": target},
                device_id_type=MESH,
            ).start()

    @pl.when(holds)
    def _():
        held[pl.ds(tiles * units, units)] = jnp.zeros((units, 2, LANES), BF16)
        held[pl.ds(me * units, units)] = outgoing[piece]
        everything = held.at[pl.ds(0, (tiles - 1) * units)]
        pltpu.make_async_copy(everything, everything, recv_a).wait()
        q = lax.rem(lane_ids((2, LANES)), level.pitch)
        left_lanes = q < 3
        own_lanes = q < level.side + 3
        first_lanes = lax.rem(q, 6) < 3

        @pl.loop(0, tiles)
        def _(k):
            target = lax.rem(me + k, tiles)
            base = [table_ref[target * 9 + band] * units for band in range(8)]
            above = table_ref[target * 9 + 8] * edge
            for unit in range(edge):
                for first, offset, place in ((0, edge + unit, unit), (5, above + unit, edge + unit)):
                    left = held[base[first] + offset].astype(F32)
                    own = held[base[first + 1] + offset].astype(F32)
                    right = held[base[first + 2] + offset].astype(F32)
                    row = jnp.where(left_lanes, left, jnp.where(own_lanes, own, right))
                    picked[target, place] = row.astype(BF16)
            for unit in range(2 * edge, units):
                left = held[base[3] + unit].astype(F32)
                right = held[base[4] + unit].astype(F32)
                picked[target, unit] = jnp.where(first_lanes, right, left).astype(BF16)

            @pl.when(k > 0)
            def _():
                pltpu.make_async_remote_copy(
                    src_ref=picked.at[target],
                    dst_ref=got.at[piece],
                    send_sem=send_b,
                    recv_sem=recv_b,
                    device_id={"tile": target},
                    device_id_type=MESH,
                ).start()

        got[piece] = picked[me]
        others = outgoing.at[pl.ds(0, pieces - 1)]
        pltpu.make_async_copy(others, others, send_a).wait()
        arrived = got.at[pl.ds(0, pieces - 1)]
        pltpu.make_async_copy(arrived, arrived, recv_b).wait()
        gone = picked.at[pl.ds(0, tiles - 1)]
        pltpu.make_async_copy(gone, gone, send_b).wait()

    @pl.when(jnp.logical_not(holds))
    def _():
        pltpu.make_async_copy(outgoing, outgoing, send_a).wait()
        pltpu.make_async_copy(got, got, recv_b).wait()


def set_halo(level, grid, units, got, fold):
    pairs = got.shape[0]
    for unit in range(level.units):
        for p in range(pairs):
            units[unit, 2 * p : 2 * p + 2, :] = got[p, unit]
    lane = lane_ids()
    q = lax.rem(lane, level.pitch)
    side, rows, pitch, edge = level.side, level.rows, level.pitch, level.edge_units
    for unit in range(level.side_units):
        value = units[2 * edge + unit].astype(F32)
        for slot in range(level.slots):
            j = unit * level.slots + slot
            if j >= rows:
                continue
            own = jnp.where(q < 3, roll(value, -6 * slot - 3), grid[3 + j])
            grid[3 + j] = jnp.where(q < side + 3, own, roll(value, side + 3 - 6 * slot))
    backwards = (
        lax.broadcasted_iota(jnp.int32, (LANES, LANES), 0) + lax.broadcasted_iota(jnp.int32, (LANES, LANES), 1)
        == side + 5
    ).astype(BF16)
    above = []
    mirrored = []
    for k in range(3):
        below = roll(units[k // level.parts].astype(F32), -(k % level.parts) * pitch)
        grid[k] = jnp.where(lane < pitch, below, roll(grid[rows + k], pitch))
        row = roll(units[edge + k // level.parts].astype(F32), -(k % level.parts) * pitch)
        above.append(row)
        mirrored.append(jnp.dot(row.astype(BF16), backwards, preferred_element_type=F32))
    for k in range(3):
        top = jnp.where(fold > 0.5, mirrored[2 - k], above[k])
        top = roll(top, LANES - pitch)
        grid[rows + 3 + k] = jnp.where(lane >= LANES - pitch, top, roll(grid[3 + k], -pitch))


def depthwise(level, grid, cols_ref, first, bias_at, conv):
    rows = level.rows
    groups = grid.shape[1] // 8

    @pl.loop(0, groups)
    def _(g):
        at = pl.ds(pl.multiple_of(g * 8, 8), 8)
        cols = cols_ref[at, :]
        total = [jnp.broadcast_to(cols[:, bias_at : bias_at + 1], (8, LANES))] * rows
        for b in range(7):
            weights = [
                jnp.broadcast_to(cols[:, first + 7 * a + b : first + 7 * a + b + 1], (8, LANES)) for a in range(7)
            ]
            for j in range(rows + 6):
                shifted = roll(grid[j, at, :], -b)
                for a in range(7):
                    if 0 <= j - a < rows:
                        total[j - a] = total[j - a] + weights[a] * shifted
        for j in range(rows):
            conv[j, at, :] = total[j]


def swap(ways, count, source, target, send, recv):
    me = lax.axis_index("chan")
    copies = []
    for k in range(1, ways):
        peer = lax.rem(me + k, ways)
        copy = pltpu.make_async_remote_copy(
            src_ref=source.at[peer],
            dst_ref=target.at[me],
            send_sem=send.at[k],
            recv_sem=recv.at[k],
            device_id={"chan": peer},
            device_id_type=MESH,
        )
        copy.start()
        copies.append(copy)
    target[me] = source[me]
    for copy in copies:
        copy.wait()


def mix(lev, every, tall_ref, up_ref, upb_ref, down_ref, branch):
    ways, count, chans, _ = every.shape
    hidden_size = up_ref.shape[1]
    step = 256

    @pl.loop(0, count // 2)
    def _(i):
        sides = []
        for jj in range(2):
            values = every[:, 2 * i + jj].astype(F32).reshape(ways * chans, LANES)
            mean = jnp.sum(values, axis=0, keepdims=True) * (1.0 / (ways * chans))
            centred = values - mean
            spread = jnp.sum(centred * centred, axis=0, keepdims=True) * (1.0 / (ways * chans))
            scaled = centred * lax.rsqrt(spread + norm_eps)
            sides.append((scaled * tall_ref[:, lev : lev + 1] + tall_ref[:, 2 + lev : 3 + lev]).astype(BF16))
        normed = jnp.concatenate(sides, axis=1)
        total = jnp.broadcast_to(tall_ref[:, 4 + lev : 5 + lev], (ways * chans, 2 * LANES))
        for h in range(hidden_size // step):
            at = slice(h * step, (h + 1) * step)
            hidden = jnp.dot(up_ref[lev, at, :], normed, preferred_element_type=F32) + upb_ref[at, lev : lev + 1]
            hidden = 0.5 * hidden * (1.0 + lax.erf(hidden * (0.5**0.5)))
            total = total + jnp.dot(down_ref[lev, :, at], hidden.astype(BF16), preferred_element_type=F32)
        for jj in range(2):
            half = total[:, jj * LANES : (jj + 1) * LANES]
            branch[:, 2 * i + jj] = half.reshape(ways, chans, LANES).astype(BF16)


def step_kernel(
    tiles,
    ways,
    table_ref,
    fold_ref,
    features_ref,
    mask_ref,
    mask1_ref,
    cols_ref,
    tall_ref,
    up_ref,
    upb_ref,
    down_ref,
    out_ref,
    grid0,
    grid1,
    units0,
    units1,
    outgoing0,
    outgoing1,
    held0,
    held1,
    picked0,
    picked1,
    got0,
    got1,
    conv,
    sent0,
    sent1,
    every0,
    every1,
    branch0,
    branch1,
    back0,
    back1,
    fine,
    flat,
    sems,
    swaps,
):
    me = lax.axis_index("tile")
    chan = lax.axis_index("chan")
    pieces = outgoing0.shape[0]
    piece = (me * pieces + tiles - 1) // tiles
    holds = jnp.logical_and(piece < pieces, (piece * tiles) // pieces == me)
    barrier = pltpu.get_barrier_semaphore()
    for k in range(1, ways):
        pl.semaphore_signal(barrier, inc=1, device_id={"chan": lax.rem(chan + k, ways)}, device_id_type=MESH)

    @pl.when(holds)
    def _():
        @pl.loop(1, tiles)
        def _(k):
            pl.semaphore_signal(barrier, inc=1, device_id={"tile": lax.rem(me + k, tiles)}, device_id_type=MESH)

    @pl.when(jnp.logical_not(holds))
    def _():
        @pl.loop(0, pieces)
        def _(p):
            pl.semaphore_signal(barrier, inc=1, device_id={"tile": (p * tiles) // pieces}, device_id_type=MESH)

    lane = lane_ids()
    half = TILE * TILE // 2
    flat[...] = features_ref[...].astype(F32)
    for j in range(FINE.rows):
        grid0[3 + j] = jnp.zeros(grid0.shape[1:], F32)
        grid0[3 + j, :, 3 : 3 + TILE] = flat[:, TILE * j : TILE * (j + 1)]
        grid0[3 + j, :, 67 : 67 + TILE] = flat[:, half + TILE * j : half + TILE * (j + 1)]
    cut_units(FINE, grid0, units0, outgoing0)

    @pl.when(holds)
    def _():
        pl.semaphore_wait(barrier, tiles - 1 + ways - 1)

    @pl.when(jnp.logical_not(holds))
    def _():
        pl.semaphore_wait(barrier, pieces + ways - 1)

    fold = fold_ref[...]
    route(FINE, tiles, table_ref, outgoing0, held0, picked0, got0, sems.at[0], sems.at[1], sems.at[2], sems.at[3])
    set_halo(FINE, grid0, units0, got0, fold)
    depthwise(FINE, grid0, cols_ref, 16, 0, conv)
    per = MIX_ROWS[0]
    for j in range(FINE.rows):
        sent0[j // per, j % per] = conv[j].astype(BF16)
    swap(ways, per, sent0, every0, swaps.at[0], swaps.at[1])
    mix(0, every0, tall_ref, up_ref, upb_ref, down_ref, branch0)
    swap(ways, per, branch0, back0, swaps.at[2], swaps.at[3])
    scale = cols_ref[:, 2:3]
    for j in range(FINE.rows):
        value = roll(grid0[3 + j], -3) + scale * back0[j // per, j % per].astype(F32)
        fine[j] = (mask_ref[j] * value).astype(BF16)

    source = lax.broadcasted_iota(jnp.int32, (2 * LANES, LANES), 0)
    target = lax.broadcasted_iota(jnp.int32, (2 * LANES, LANES), 1)
    block = lax.rem(source, LANES)
    wanted = 64 * (block // 64) + 32 * (source // LANES) + lax.rem(block, 64) // 2 + 3
    gather = jnp.logical_and(
        target == wanted, jnp.logical_and(lax.rem(block, 2) == 0, lax.rem(block, 64) < TILE)
    ).astype(BF16)
    pool = [cols_ref[:, 4 + t : 5 + t] for t in range(4)]
    for j in range(COARSE.rows):
        sides = []
        for row in (j, j + COARSE.rows):
            low = fine[2 * row].astype(F32)
            high = fine[2 * row + 1].astype(F32)
            value = pool[0] * low + pool[1] * roll(low, -1) + pool[2] * high + pool[3] * roll(high, -1)
            sides.append(value.astype(BF16))
        grid1[3 + j] = jnp.dot(jnp.concatenate(sides, axis=1), gather, preferred_element_type=F32)
    cut_units(COARSE, grid1, units1, outgoing1)
    route(COARSE, tiles, table_ref, outgoing1, held1, picked1, got1, sems.at[4], sems.at[5], sems.at[6], sems.at[7])
    set_halo(COARSE, grid1, units1, got1, fold)
    depthwise(COARSE, grid1, cols_ref, 65, 1, conv)
    per = MIX_ROWS[1]
    for j in range(ways * per):
        if j < COARSE.rows:
            sent1[j // per, j % per] = conv[j].astype(BF16)
        else:
            sent1[j // per, j % per] = jnp.zeros(sent1.shape[2:], BF16)
    swap(ways, per, sent1, every1, swaps.at[4], swaps.at[5])
    mix(1, every1, tall_ref, up_ref, upb_ref, down_ref, branch1)
    swap(ways, per, branch1, back1, swaps.at[6], swaps.at[7])
    scale = cols_ref[:, 3:4]
    source = lax.broadcasted_iota(jnp.int32, (LANES, LANES), 0)
    target = lax.broadcasted_iota(jnp.int32, (LANES, LANES), 1)
    odd = lax.rem(lane, 2) == 1
    spread = [jnp.where(odd, cols_ref[:, 9 + 2 * t : 10 + 2 * t], cols_ref[:, 8 + 2 * t : 9 + 2 * t]) for t in range(2)]
    for j in range(COARSE.rows):
        value = roll(grid1[3 + j], -3) + scale * back1[j // per, j % per].astype(F32)
        coarse = (mask1_ref[j] * value).astype(BF16)
        for t in range(2):
            wanted = 64 * (target // 64) + 32 * t + lax.rem(target, 64) // 2
            scatter = jnp.logical_and(source == wanted, lax.rem(target, 64) < TILE).astype(BF16)
            wide = jnp.dot(coarse, scatter, preferred_element_type=F32)
            for row in range(2):
                at = 2 * (j + COARSE.rows * t) + row
                value = mask_ref[at] * (fine[at].astype(F32) + spread[row] * wide)
                flat[:, TILE * at : TILE * (at + 1)] = value[:, :TILE]
                flat[:, half + TILE * at : half + TILE * (at + 1)] = value[:, 64 : 64 + TILE]
    out_ref[...] = flat[...].astype(BF16)


def per_device(
    ways,
    features,
    land_mask,
    wet_slots,
    device_of,
    depth_weight,
    depth_bias,
    norm_gain,
    norm_bias,
    up_weight,
    up_bias,
    down_weight,
    down_bias,
    layer_scale,
    pool_weight,
    spread_weight,
):
    tiles = wet_slots.shape[0]
    chans = features.shape[1]
    table = source_table(wet_slots, device_of, 2 * tiles // GRID_Y, GRID_Y)
    fold = lax.dynamic_slice(table, (lax.axis_index("tile"), 8), (1, 1)).astype(F32)
    fold = jnp.broadcast_to(fold, (1, LANES))
    cells = land_mask[0].astype(F32).reshape(2, 24, TILE)
    mask = jnp.pad(cells, ((0, 0), (0, 0), (0, 16))).transpose(1, 0, 2).reshape(24, 1, LANES)
    small = jnp.max(land_mask[0].reshape(24, 2, 24, 2), axis=(1, 3)).astype(F32).reshape(4, 6, 24)
    mask1 = jnp.pad(small, ((0, 0), (0, 0), (0, 8))).transpose(1, 0, 2).reshape(6, 1, LANES)
    cols = jnp.concatenate(
        [
            depth_bias.T,
            layer_scale.T,
            pool_weight,
            spread_weight,
            jnp.zeros((chans, 4), F32),
            depth_weight[0],
            depth_weight[1],
            jnp.zeros((chans, 14), F32),
        ],
        axis=1,
    )
    tall = jnp.concatenate([norm_gain, norm_bias, down_bias, jnp.zeros((2, norm_gain.shape[1]), F32)], axis=0).T
    pairs = chans // 2
    scratch = [
        pltpu.VMEM((FINE.rows + 6, chans, LANES), F32),
        pltpu.VMEM((COARSE.rows + 6, chans, LANES), F32),
    ]
    scratch += [pltpu.VMEM((level.units, chans, LANES), BF16) for level in (FINE, COARSE)]
    scratch += [pltpu.VMEM((pairs, level.units, 2, LANES), BF16) for level in (FINE, COARSE)]
    scratch += [pltpu.VMEM(((tiles + 1) * level.units, 2, LANES), BF16) for level in (FINE, COARSE)]
    scratch += [pltpu.VMEM((tiles, level.units, 2, LANES), BF16) for level in (FINE, COARSE)]
    scratch += [pltpu.VMEM((pairs, level.units, 2, LANES), BF16) for level in (FINE, COARSE)]
    scratch += [pltpu.VMEM((FINE.rows, chans, LANES), F32)]
    scratch += [pltpu.VMEM((ways, per, chans, LANES), BF16) for _ in range(4) for per in MIX_ROWS]
    scratch += [pltpu.VMEM((FINE.rows, chans, LANES), BF16), pltpu.VMEM((chans, TILE * TILE), F32)]
    scratch += [pltpu.SemaphoreType.DMA((8,)), pltpu.SemaphoreType.DMA((8, ways))]
    out = pl.pallas_call(
        functools.partial(step_kernel, tiles, ways),
        out_shape=jax.ShapeDtypeStruct(features.shape[1:], BF16),
        in_specs=[SMEM_SPEC] + [VMEM_SPEC] * 9,
        out_specs=VMEM_SPEC,
        scratch_shapes=scratch,
        compiler_params=pltpu.CompilerParams(
            collective_id=0, has_side_effects=True, vmem_limit_bytes=48 * 1024 * 1024
        ),
        name="ocean_step",
    )(table.reshape(-1), fold, features[0], mask, mask1, cols, tall, up_weight, up_bias.T, down_weight)
    return out[None]


def solution(mesh):
    placed = (
        P("tile", "chan", None),
        P("tile", None),
        P(),
        P(),
        P(None, "chan", None),
        P(None, "chan"),
        P(),
        P(),
        P(),
        P(),
        P(),
        P(),
        P(None, "chan"),
        P("chan", None),
        P("chan", None),
    )
    return jax.shard_map(
        functools.partial(per_device, mesh.shape["chan"]),
        mesh=mesh,
        in_specs=placed,
        out_specs=P("tile", "chan", None),
        check_vma=False,
    )
```

time: 146 us -> 91.5 us (0.63)
  local copies, waits for them, and re-layouts: 35.7 us -> 8.13 us
  other arithmetic: 22.2 us -> 4.43 us
  Pallas kernels: 85.8 us -> 77.2 us
    another operation x52 -> x1, local copies, waits for them, and re-layouts: 13.1 us -> 0.53 us  [per_device(): land_mask[0].reshape(24, 2, 24, 2)]
    add x3 -> x1, other arithmetic: 10.5 us -> 0.01 us  [source_table(): device_of[None, None, :] + 1]
    slice x21 -> x0, local copies, waits for them, and re-layouts: 8.93 us -> none  [the longest x6 3.17 us: depthwise(): weights[:, row_step * 7 + col_step][:, None]]
    pallas_call x4 -> x1, Pallas kernels: 85.8 us -> 77.2 us  [per_device(): pl.pallas_call(functools.partial(step_kernel, tiles, ways), out_shape=jax...]
    convert_element_type x7 -> x3, local copies, waits for them, and re-layouts: 4.16 us -> 0.09 us  [the longest x2 0.09 us: per_device(): cells = land_mask[0].astype(F32).reshape(2, 24, TILE)]
    convert_element_type x12 -> x3, other arithmetic: 4 us -> 0.05 us  [the longest x1 0.03 us: per_device(): cells = land_mask[0].astype(F32).reshape(2, 24, TILE)]
    select_n x8 -> x4, other arithmetic: 3.37 us -> 0.11 us  [the longest x1 0.08 us: source_table(): jnp.where(near_row < 0, -1, source_row * grid_x + source_column)]
    unnamed x49 -> x37, local copies, waits for them, and re-layouts: 3.84 us -> 5.94 us
where the time goes in v1:
time: 91.5 us; the launch traced here: 90.6 us
  Pallas kernels  77.2 us (84%)
  local copies, waits for them, and re-layouts  8.13 us (9%)
  other arithmetic  4.43 us (5%)
    pallas_call x1, Pallas kernels, per_device(): pl.pallas_call(functools.partial(step_kernel, tiles, ways), out_shape=jax...  77.2 us
    unnamed x37, local copies, waits for them, and re-layouts  5.94 us
    reduce_sum x1, other arithmetic, source_table(): jnp.sum(jnp.where(source_slot[:, :, None] == wet_slots[None, None, :], de...  2.39 us

profile of v1, /device:TPU:1, one launch (start us, length us, event | category | flops | bytes accessed | tf_op | source)
XLA Modules:
  0.0 90.6 jit_solution(427866771497699415)
XLA Ops:
  0.0 0.7 copy-done.13
  0.7 0.1 select_reduce_fusion.1
  0.8 0.6 pad_dynamic-slice_fusion
  1.6 0.6 copy-done.6
  2.5 0.1 reshape.216.mask_ref
  2.6 0.6 copy-done.11
  3.3 0.1 copy.70
  3.4 0.6 copy-done.9
  4.0 0.6 copy-done.10
  4.7 0.1 concatenate.10.cols_ref
  4.9 0.1 copy.63
  5.0 2.4 %select_reduce_fusion = s32[128,8]{1,0:T(8,128)S(1)} fusion(s32[128]{0:T(128)S(1)} %broadcast_add_fusion, s32[128]{0:T(128)S(1)} %copy-done.13, s32[128,8]{1,0:T(8,128)S(1)} %copy.63), kind=kLoop, calls=%fused_computation | loop fusion | flops 392192 | bytes 9216 | tf_op jit(solution)/shard_map/reduce_sum | solution.py:59
  7.4 1.2 %fusion.8 = s32[1,1]{0,1:T(1,128)} fusion(s32[1,1]{0,1:T(1,128)} %pad_dynamic-slice_fusion, s32[]{:T(128)S(6)} %select_n.144, s32[128,8]{0,1:T(8,128)S(1)} %add_select_fusion.2), kind=kLoop, calls=%fused_computation.47 | loop fusion | flops 1 | bytes 4108 | tf_op jit(solution)/shard_map/concatenate | solution.py:64
  9.3 0.1 copy.66
  9.4 0.2 reshape.215.table_ref
  9.6 0.1 copy.73
  9.7 0.6 copy-done.5
  10.3 0.2 copy.74
  10.5 0.5 reshape_squeeze.3
  11.0 0.5 reduce_max.9
  11.7 0.3 copy.75.up_ref
  11.9 0.8 copy-done
  12.8 77.2 %ocean_step.1 = bf16[48,2304]{1,0:T(8,128)(2,1)S(1)} custom-call(s32[1152]{0:T(1024)S(1)} %reshape.215.table_ref, f32[1,128]{1,0:T(1,128)S(1)} %broadcast_in_dim.103.fold_ref, bf16[48,2304]{1,0:T(8,128)(2,1)S(1)} %bitcast.28, f32[24,1,128]{2,1,0:T(1,128)S(1)} %reshape.216.mask_ref, f32[6,1,128]{2,1,0:T(1,128)S(1)} %reshape.217.mask1_ref, ...), custom_call_target="tpu_custom_call" | custom-call | tf_op jit(solution)/shard_map/ocean_step/pallas_call | solution.py:483
  89.9 0.7 copy.77
  (52 shorter events, 1.0 us)
Async XLA Ops:
  0.0 0.7 copy-start.13
  0.0 0.7 copy-start.14
  1.5 0.7 copy-start.6
  1.5 0.7 copy-start.7
  1.5 0.7 copy-start.8
  1.5 0.8 copy-start.4
  2.5 0.7 copy-start.11
  2.5 0.8 copy-start.12
  3.2 1.6 %copy-start.3 = (f32[2,48,49]{2,1,0:T(8,128)S(1)}, f32[2,48,49]{2,1,0:T(8,128)}, u32[]{:S(2)}) copy-start(f32[2,48,49]{2,1,0:T(8,128)} %param.19) | copy-start | bytes 56452
  3.3 0.7 copy-start.9
  3.9 0.7 copy-start.10
  9.6 0.7 copy-start.5
  10.5 1.2 %copy-start.2 = (bf16[2,768,192]{1,2,0:T(8,128)(2,1)S(1)}, bf16[2,768,192]{1,2,0:T(8,128)(2,1)}, u32[]{:S(2)}) copy-start(bf16[2,768,192]{1,2,0:T(8,128)(2,1)} %param.23) | copy-start | bytes 1769476
  11.6 1.1 %copy-start = (bf16[2,192,768]{2,1,0:T(8,128)(2,1)S(1)}, bf16[2,192,768]{2,1,0:T(8,128)(2,1)}, u32[]{:S(2)}) copy-start(bf16[2,192,768]{2,1,0:T(8,128)(2,1)} %down_ref.1) | copy-start | bytes 1769476
  11.7 1.1 %copy-start.1 = (bf16[1,48,2304]{2,1,0:T(8,128)(2,1)S(1)}, bf16[1,48,2304]{2,1,0:T(8,128)(2,1)}, u32[]{:S(2)}) copy-start(bf16[1,48,2304]{2,1,0:T(8,128)(2,1)} %param.15) | copy-start | bytes 663556

commit v2 on v1

v2 whole, which is shorter than its diff:
```python
import functools

import jax
import jax.numpy as jnp
from jax import lax
from jax.experimental import pallas as pl
from jax.experimental.pallas import tpu as pltpu
from jax.sharding import PartitionSpec as P

TILE = 48
GRID_Y = 4
MESH = pl.DeviceIdType.MESH
norm_eps = 1e-06
VMEM_SPEC = pl.BlockSpec(memory_space=pltpu.VMEM)
SMEM_SPEC = pl.BlockSpec(memory_space=pltpu.SMEM)
LANES = 128
F32 = jnp.float32
BF16 = jnp.bfloat16


class Level:
    def __init__(self, side, parts, slots):
        self.side = side
        self.parts = parts
        self.pitch = LANES // parts
        self.rows = side // parts
        self.slots = slots
        self.edge_units = -(-3 // parts)
        self.side_units = -(-self.rows // slots)
        self.units = max(2 * self.edge_units, self.side_units)


FINE = Level(TILE, 2, 8)
COARSE = Level(TILE // 2, 4, 3)
MIX_ROWS = (6, 2)


def roll(x, shift):
    shift %= LANES
    return x if shift == 0 else pltpu.roll(x, shift, x.ndim - 1)


def source_table(grid_x, grid_y, wet_ref, device_of_ref, table_ref):
    tiles = wet_ref.shape[1]
    wet = wet_ref[...]
    held_by = device_of_ref[...]
    device = lax.broadcasted_iota(jnp.int32, (tiles, tiles), 0)
    slot = jnp.sum(jnp.where(held_by == device, wet, 0), axis=1, keepdims=True)
    column = lax.rem(slot, grid_x)
    tile_row = lax.div(slot, grid_x)
    band = lax.broadcasted_iota(jnp.int32, (tiles, LANES), 1)
    up = jnp.where(band < 3, -1, jnp.where(band < 5, 0, 1))
    right = jnp.where(band < 3, band - 1, jnp.where(band < 5, 2 * band - 7, band - 6))
    near_row = tile_row + up
    folded = near_row >= grid_y
    right = jnp.where(folded, -right, right)
    near_column = lax.rem(column + right + grid_x, grid_x)
    source_column = jnp.where(folded, grid_x - 1 - near_column, near_column)
    source_row = jnp.where(folded, grid_y - 1, near_row)
    source_slot = jnp.where(near_row < 0, -1, source_row * grid_x + source_column)
    table = jnp.where(tile_row >= grid_y - 1, 1, jnp.zeros((tiles, LANES), jnp.int32))
    fold = jnp.where(device[:, :1] == lax.axis_index("tile"), table, 0)
    fold = jnp.sum(fold.astype(F32), axis=0, keepdims=True)
    for b in range(8):
        here = source_slot[:, b : b + 1] == wet
        found = jnp.sum(jnp.where(here, held_by + 1, 0), axis=1, keepdims=True)
        found = jnp.where(found > 0, found - 1, tiles)
        table = jnp.where(band == b, found, table)
    table_ref[...] = table
    return fold


def lane_ids(shape=(1, LANES)):
    return lax.broadcasted_iota(jnp.int32, shape, len(shape) - 1)


def cut_units(level, grid, units, outgoing):
    lane = lane_ids()
    q = lax.rem(lane, level.pitch)
    part = lane // level.pitch
    side, rows, pitch = level.side, level.rows, level.pitch

    def periodic(j):
        own = grid[j]
        own = jnp.where(q < 3, roll(own, -side), own)
        return jnp.where(q >= side + 3, roll(own, side), own)

    for edge in range(2):
        at = 0 if edge == 0 else level.parts - 1
        for unit in range(level.edge_units):
            value = None
            for k in range(3):
                if k // level.parts != unit:
                    continue
                row = roll(periodic((3 if edge == 0 else rows) + k), (k % level.parts - at) * pitch)
                value = row if value is None else jnp.where(part == k % level.parts, row, value)
            units[0, edge * level.edge_units + unit] = value.astype(BF16)
    for unit in range(level.side_units):
        value = None
        for slot in range(level.slots):
            j = unit * level.slots + slot
            if j >= rows:
                continue
            own = grid[3 + j]
            both = jnp.where(q < 6 * slot + 3, roll(own, 6 * slot - 3), roll(own, 6 * slot + 3 - side))
            value = both if value is None else jnp.where(q < 6 * slot, value, both)
        units[1, unit] = value.astype(BF16)
    for role in range(2):
        for unit in range((2 * level.edge_units, level.side_units)[role]):
            for p in range(outgoing.shape[0] // 2):
                outgoing[2 * p + role, unit] = units[role, unit, 2 * p : 2 * p + 2, :]


def scatter_strips(level, tiles, outgoing, held, send_a, recv_a):
    me = lax.axis_index("tile")
    pieces = outgoing.shape[0]
    units = level.units

    @pl.loop(0, pieces)
    def _(p):
        target = (p * tiles) // pieces

        @pl.when(target != me)
        def _():
            pltpu.make_async_remote_copy(
                src_ref=outgoing.at[p],
                dst_ref=held.at[pl.ds(me * units, units)],
                send_sem=send_a,
                recv_sem=recv_a,
                device_id={"tile": target},
                device_id_type=MESH,
            ).start()


def route(level, tiles, table_ref, outgoing, held, picked, got, send_a, recv_a, send_b, recv_b):
    me = lax.axis_index("tile")
    pieces = outgoing.shape[0]
    piece = (me * pieces + tiles - 1) // tiles
    holds = jnp.logical_and(piece < pieces, (piece * tiles) // pieces == me)
    units, edge = level.units, level.edge_units

    def send(target, k):
        @pl.when(k > 0)
        def _():
            pltpu.make_async_remote_copy(
                src_ref=picked.at[target],
                dst_ref=got.at[piece],
                send_sem=send_b,
                recv_sem=recv_b,
                device_id={"tile": target},
                device_id_type=MESH,
            ).start()

    @pl.when(holds)
    def _():
        held[pl.ds(tiles * units, units)] = jnp.zeros((units, 2, LANES), BF16)
        held[pl.ds(me * units, units)] = outgoing[piece]
        everything = held.at[pl.ds(0, (tiles - 1) * units)]
        pltpu.make_async_copy(everything, everything, recv_a).wait()
        q = lax.rem(lane_ids((2, LANES)), level.pitch)
        left_lanes = q < 3
        own_lanes = q < level.side + 3
        first_lanes = lax.rem(q, 6) < 3

        @pl.when(lax.rem(piece, 2) == 0)
        def _():
            @pl.loop(0, tiles)
            def _(k):
                target = lax.rem(me + k, tiles)
                below = [table_ref[target, band] * units + edge for band in range(3)]
                fold = table_ref[target, 8] * edge
                above = [table_ref[target, band] * units + fold for band in range(5, 8)]
                for unit in range(edge):
                    for base, place in ((below, unit), (above, edge + unit)):
                        left = held[base[0] + unit].astype(F32)
                        own = held[base[1] + unit].astype(F32)
                        right = held[base[2] + unit].astype(F32)
                        row = jnp.where(left_lanes, left, jnp.where(own_lanes, own, right))
                        picked[target, place] = row.astype(BF16)
                send(target, k)

        @pl.when(lax.rem(piece, 2) == 1)
        def _():
            @pl.loop(0, tiles)
            def _(k):
                target = lax.rem(me + k, tiles)
                at_left = table_ref[target, 3] * units
                at_right = table_ref[target, 4] * units
                for unit in range(level.side_units):
                    left = held[at_left + unit].astype(F32)
                    right = held[at_right + unit].astype(F32)
                    picked[target, unit] = jnp.where(first_lanes, right, left).astype(BF16)
                send(target, k)

        got[piece] = picked[me]
        others = outgoing.at[pl.ds(0, pieces - 1)]
        pltpu.make_async_copy(others, others, send_a).wait()
        arrived = got.at[pl.ds(0, pieces - 1)]
        pltpu.make_async_copy(arrived, arrived, recv_b).wait()
        gone = picked.at[pl.ds(0, tiles - 1)]
        pltpu.make_async_copy(gone, gone, send_b).wait()

    @pl.when(jnp.logical_not(holds))
    def _():
        pltpu.make_async_copy(outgoing, outgoing, send_a).wait()
        pltpu.make_async_copy(got, got, recv_b).wait()


def set_halo(level, grid, units, got, fold):
    for role in range(2):
        for unit in range((2 * level.edge_units, level.side_units)[role]):
            for p in range(got.shape[0] // 2):
                units[role, unit, 2 * p : 2 * p + 2, :] = got[2 * p + role, unit]
    lane = lane_ids()
    q = lax.rem(lane, level.pitch)
    side, rows, pitch, edge = level.side, level.rows, level.pitch, level.edge_units
    for unit in range(level.side_units):
        value = units[1, unit].astype(F32)
        for slot in range(level.slots):
            j = unit * level.slots + slot
            if j >= rows:
                continue
            own = jnp.where(q < 3, roll(value, -6 * slot - 3), grid[3 + j])
            grid[3 + j] = jnp.where(q < side + 3, own, roll(value, side + 3 - 6 * slot))
    backwards = (
        lax.broadcasted_iota(jnp.int32, (LANES, LANES), 0) + lax.broadcasted_iota(jnp.int32, (LANES, LANES), 1)
        == side + 5
    ).astype(BF16)
    above = []
    mirrored = []
    for k in range(3):
        below = roll(units[0, k // level.parts].astype(F32), -(k % level.parts) * pitch)
        grid[k] = jnp.where(lane < pitch, below, roll(grid[rows + k], pitch))
        row = roll(units[0, edge + k // level.parts].astype(F32), -(k % level.parts) * pitch)
        above.append(row)
        mirrored.append(jnp.dot(row.astype(BF16), backwards, preferred_element_type=F32))
    for k in range(3):
        top = jnp.where(fold > 0.5, mirrored[2 - k], above[k])
        top = roll(top, LANES - pitch)
        grid[rows + 3 + k] = jnp.where(lane >= LANES - pitch, top, roll(grid[3 + k], -pitch))


def start_swap(ways, source, target, send, recv, window):
    me = lax.axis_index("chan")
    for k in range(1, ways):
        peer = lax.rem(me + k, ways)
        pltpu.make_async_remote_copy(
            src_ref=source.at[(peer,) + window],
            dst_ref=target.at[(me,) + window],
            send_sem=send.at[k],
            recv_sem=recv.at[k],
            device_id={"chan": peer},
            device_id_type=MESH,
        ).start()


def finish_swap(ways, source, target, send, recv):
    me = lax.axis_index("chan")
    target[me] = source[me]
    for k in range(1, ways):
        block = source.at[k]
        pltpu.make_async_copy(block, block, send.at[k]).wait()
        pltpu.make_async_copy(block, block, recv.at[k]).wait()


def depthwise(level, lev, grid, taps_ref, cols, conv, sent, every, send, recv):
    rows = level.rows
    ways, per = sent.shape[:2]
    wide = 16
    for j in range(rows, ways * per):
        sent[j // per, j % per] = jnp.zeros(sent.shape[2:], BF16)

    @pl.loop(0, grid.shape[1] // wide)
    def _(g):
        both = pl.ds(pl.multiple_of(g * wide, wide), wide)
        for part in range(2):
            at = pl.ds(pl.multiple_of(g * wide + part * 8, 8), 8)
            taps = taps_ref[lev, at, :]
            total = [jnp.broadcast_to(cols[at, lev : lev + 1], (8, LANES))] * rows
            for b in range(7):
                weights = [jnp.broadcast_to(taps[:, 7 * a + b : 7 * a + b + 1], (8, LANES)) for a in range(7)]
                for j in range(rows + 6):
                    shifted = roll(grid[j, at, :], -b)
                    for a in range(7):
                        if 0 <= j - a < rows:
                            total[j - a] = total[j - a] + weights[a] * shifted
            for j in range(rows):
                conv[j, at, :] = total[j]
        for j in range(rows):
            sent[j // per, j % per, both, :] = conv[j, both, :].astype(BF16)
        start_swap(ways, sent, every, send, recv, (slice(None), both))

    finish_swap(ways, sent, every, send, recv)


def mix(lev, every, tall_ref, up_ref, upb_ref, down_ref, branch, back, send, recv):
    ways, count, chans, _ = every.shape
    hidden_size = up_ref.shape[1]
    step = 256

    @pl.loop(0, count // 2)
    def _(i):
        sides = []
        for jj in range(2):
            values = every[:, 2 * i + jj].astype(F32).reshape(ways * chans, LANES)
            mean = jnp.sum(values, axis=0, keepdims=True) * (1.0 / (ways * chans))
            centred = values - mean
            spread = jnp.sum(centred * centred, axis=0, keepdims=True) * (1.0 / (ways * chans))
            scaled = centred * lax.rsqrt(spread + norm_eps)
            sides.append((scaled * tall_ref[:, lev : lev + 1] + tall_ref[:, 2 + lev : 3 + lev]).astype(BF16))
        normed = jnp.concatenate(sides, axis=1)
        total = jnp.broadcast_to(tall_ref[:, 4 + lev : 5 + lev], (ways * chans, 2 * LANES))
        for h in range(hidden_size // step):
            at = slice(h * step, (h + 1) * step)
            hidden = jnp.dot(up_ref[lev, at, :], normed, preferred_element_type=F32) + upb_ref[at, lev : lev + 1]
            hidden = 0.5 * hidden * (1.0 + lax.erf(hidden * (0.5**0.5)))
            total = total + jnp.dot(down_ref[lev, :, at], hidden.astype(BF16), preferred_element_type=F32)
        for jj in range(2):
            half = total[:, jj * LANES : (jj + 1) * LANES]
            branch[:, 2 * i + jj] = half.reshape(ways, chans, LANES).astype(BF16)
        start_swap(ways, branch, back, send, recv, (pl.ds(2 * i, 2),))

    finish_swap(ways, branch, back, send, recv)


def columns(block):
    return jnp.transpose(block)


def step_kernel(
    tiles,
    ways,
    wet_ref,
    device_of_ref,
    features_ref,
    land_ref,
    taps_ref,
    bias_ref,
    gain_ref,
    shift_ref,
    up_ref,
    up_bias_ref,
    down_ref,
    down_bias_ref,
    scale_ref,
    pool_ref,
    spread_ref,
    out_ref,
    table_v,
    table_s,
    rows_a,
    rows_b,
    rows_c,
    cols,
    tall,
    upb,
    mask,
    mask1,
    gather,
    grid0,
    grid1,
    units0,
    units1,
    outgoing0,
    outgoing1,
    held0,
    held1,
    picked0,
    picked1,
    got0,
    got1,
    conv,
    sent0,
    sent1,
    every0,
    every1,
    branch0,
    branch1,
    back0,
    back1,
    fine,
    flat,
    sems,
    swaps,
):
    me = lax.axis_index("tile")
    chan = lax.axis_index("chan")
    pieces = outgoing0.shape[0]
    chans = grid0.shape[1]
    piece = (me * pieces + tiles - 1) // tiles
    holds = jnp.logical_and(piece < pieces, (piece * tiles) // pieces == me)
    barrier = pltpu.get_barrier_semaphore()

    @pl.when(holds)
    def _():
        @pl.loop(1, tiles)
        def _(k):
            pl.semaphore_signal(barrier, inc=1, device_id={"tile": lax.rem(me + k, tiles)}, device_id_type=MESH)

    @pl.when(jnp.logical_not(holds))
    def _():
        @pl.loop(0, pieces)
        def _(p):
            pl.semaphore_signal(barrier, inc=1, device_id={"tile": (p * tiles) // pieces}, device_id_type=MESH)

    for k in range(1, ways):
        pl.semaphore_signal(barrier, inc=1, device_id={"chan": lax.rem(chan + k, ways)}, device_id_type=MESH)

    lane = lane_ids()
    half = TILE * TILE // 2
    flat[...] = features_ref[...].astype(F32)
    for j in range(FINE.rows):
        grid0[3 + j] = jnp.zeros(grid0.shape[1:], F32)
        grid0[3 + j, :, 3 : 3 + TILE] = flat[:, TILE * j : TILE * (j + 1)]
        grid0[3 + j, :, 67 : 67 + TILE] = flat[:, half + TILE * j : half + TILE * (j + 1)]
    for outgoing in (outgoing0, outgoing1):
        outgoing[...] = jnp.zeros(outgoing.shape, BF16)
    cut_units(FINE, grid0, units0, outgoing0)

    @pl.when(holds)
    def _():
        pl.semaphore_wait(barrier, tiles - 1 + ways - 1)

    @pl.when(jnp.logical_not(holds))
    def _():
        pl.semaphore_wait(barrier, pieces + ways - 1)

    scatter_strips(FINE, tiles, outgoing0, held0, sems.at[0], sems.at[1])

    fold = source_table(2 * tiles // GRID_Y, GRID_Y, wet_ref, device_of_ref, table_v)
    table_copy = pltpu.make_async_copy(table_v, table_s, sems.at[8])
    table_copy.start()
    rows_a[...] = jnp.zeros(rows_a.shape, F32)
    for at, ref in ((0, bias_ref), (2, scale_ref), (4, pool_ref), (8, spread_ref)):
        rows_a[at : at + ref.shape[0], :chans] = ref[...]
    cols[...] = columns(rows_a[...])[:chans]
    rows_b[...] = jnp.zeros(rows_b.shape, F32)
    for at, ref in ((0, gain_ref), (2, shift_ref), (4, down_bias_ref)):
        rows_b[at : at + 2, : ways * chans] = ref[...]
    tall[...] = columns(rows_b[...])[: ways * chans]
    rows_c[...] = jnp.zeros(rows_c.shape, F32)
    rows_c[0:2, :] = up_bias_ref[...]
    upb[...] = columns(rows_c[...])
    flat[0:1, :] = land_ref[...].astype(F32)
    for j in range(FINE.rows):
        mask[j] = jnp.zeros((1, LANES), F32)
        mask[j, :, :TILE] = flat[0:1, TILE * j : TILE * (j + 1)]
        mask[j, :, 64 : 64 + TILE] = flat[0:1, half + TILE * j : half + TILE * (j + 1)]
    source = lax.broadcasted_iota(jnp.int32, (2 * LANES, LANES), 0)
    target = lax.broadcasted_iota(jnp.int32, (2 * LANES, LANES), 1)
    block = lax.rem(source, LANES)
    wanted = 64 * (block // 64) + 32 * (source // LANES) + lax.rem(block, 64) // 2 + 3
    gather[...] = jnp.logical_and(
        target == wanted, jnp.logical_and(lax.rem(block, 2) == 0, lax.rem(block, 64) < TILE)
    ).astype(BF16)
    for j in range(COARSE.rows):
        sides = []
        for row in (j, j + COARSE.rows):
            value = jnp.broadcast_to(jnp.maximum(mask[2 * row], mask[2 * row + 1]), (8, LANES))
            sides.append(jnp.maximum(value, roll(value, -1)).astype(BF16))
        value = jnp.dot(jnp.concatenate(sides, axis=1), gather[...], preferred_element_type=F32)
        mask1[j] = roll(value, -3)[0:1]
    table_copy.wait()

    route(FINE, tiles, table_s, outgoing0, held0, picked0, got0, sems.at[0], sems.at[1], sems.at[2], sems.at[3])
    set_halo(FINE, grid0, units0, got0, fold)
    depthwise(FINE, 0, grid0, taps_ref, cols, conv, sent0, every0, swaps.at[0], swaps.at[1])
    mix(0, every0, tall, up_ref, upb, down_ref, branch0, back0, swaps.at[2], swaps.at[3])
    per = MIX_ROWS[0]
    scale = cols[:, 2:3]
    for j in range(FINE.rows):
        value = roll(grid0[3 + j], -3) + scale * back0[j // per, j % per].astype(F32)
        fine[j] = (mask[j] * value).astype(BF16)
    pool = [cols[:, 4 + t : 5 + t] for t in range(4)]
    for j in range(COARSE.rows):
        sides = []
        for row in (j, j + COARSE.rows):
            low = fine[2 * row].astype(F32)
            high = fine[2 * row + 1].astype(F32)
            value = pool[0] * low + pool[1] * roll(low, -1) + pool[2] * high + pool[3] * roll(high, -1)
            sides.append(value.astype(BF16))
        grid1[3 + j] = jnp.dot(jnp.concatenate(sides, axis=1), gather[...], preferred_element_type=F32)
    cut_units(COARSE, grid1, units1, outgoing1)
    scatter_strips(COARSE, tiles, outgoing1, held1, sems.at[4], sems.at[5])
    route(COARSE, tiles, table_s, outgoing1, held1, picked1, got1, sems.at[4], sems.at[5], sems.at[6], sems.at[7])
    set_halo(COARSE, grid1, units1, got1, fold)
    depthwise(COARSE, 1, grid1, taps_ref, cols, conv, sent1, every1, swaps.at[4], swaps.at[5])
    mix(1, every1, tall, up_ref, upb, down_ref, branch1, back1, swaps.at[6], swaps.at[7])
    per = MIX_ROWS[1]
    scale = cols[:, 3:4]
    source = lax.broadcasted_iota(jnp.int32, (LANES, LANES), 0)
    target = lax.broadcasted_iota(jnp.int32, (LANES, LANES), 1)
    odd = lax.rem(lane, 2) == 1
    spread = [jnp.where(odd, cols[:, 9 + 2 * t : 10 + 2 * t], cols[:, 8 + 2 * t : 9 + 2 * t]) for t in range(2)]
    for j in range(COARSE.rows):
        value = roll(grid1[3 + j], -3) + scale * back1[j // per, j % per].astype(F32)
        coarse = (mask1[j] * value).astype(BF16)
        for t in range(2):
            wanted = 64 * (target // 64) + 32 * t + lax.rem(target, 64) // 2
            scatter = jnp.logical_and(source == wanted, lax.rem(target, 64) < TILE).astype(BF16)
            wide = jnp.dot(coarse, scatter, preferred_element_type=F32)
            for row in range(2):
                at = 2 * (j + COARSE.rows * t) + row
                value = mask[at] * (fine[at].astype(F32) + spread[row] * wide)
                flat[:, TILE * at : TILE * (at + 1)] = value[:, :TILE]
                flat[:, half + TILE * at : half + TILE * (at + 1)] = value[:, 64 : 64 + TILE]
    out_ref[...] = flat[...].astype(BF16)


def per_device(
    ways,
    features,
    land_mask,
    wet_slots,
    device_of,
    depth_weight,
    depth_bias,
    norm_gain,
    norm_bias,
    up_weight,
    up_bias,
    down_weight,
    down_bias,
    layer_scale,
    pool_weight,
    spread_weight,
):
    tiles = wet_slots.shape[0]
    chans = features.shape[1]
    levels = (FINE, COARSE)
    scratch = [
        pltpu.VMEM((tiles, LANES), jnp.int32),
        pltpu.SMEM((tiles, LANES), jnp.int32),
        pltpu.VMEM((16, LANES), F32),
        pltpu.VMEM((8, 2 * LANES), F32),
        pltpu.VMEM((8, up_bias.shape[1]), F32),
        pltpu.VMEM((chans, 16), F32),
        pltpu.VMEM((ways * chans, 8), F32),
        pltpu.VMEM((up_bias.shape[1], 8), F32),
        pltpu.VMEM((FINE.rows, 1, LANES), F32),
        pltpu.VMEM((COARSE.rows, 1, LANES), F32),
        pltpu.VMEM((2 * LANES, LANES), BF16),
        pltpu.VMEM((FINE.rows + 6, chans, LANES), F32),
        pltpu.VMEM((COARSE.rows + 6, chans, LANES), F32),
    ]
    scratch += [pltpu.VMEM((2, level.units, chans, LANES), BF16) for level in levels]
    scratch += [pltpu.VMEM((chans, level.units, 2, LANES), BF16) for level in levels]
    scratch += [pltpu.VMEM(((tiles + 1) * level.units, 2, LANES), BF16) for level in levels]
    scratch += [pltpu.VMEM((tiles, level.units, 2, LANES), BF16) for level in levels]
    scratch += [pltpu.VMEM((chans, level.units, 2, LANES), BF16) for level in levels]
    scratch += [pltpu.VMEM((FINE.rows, chans, LANES), F32)]
    scratch += [pltpu.VMEM((ways, per, chans, LANES), BF16) for _ in range(4) for per in MIX_ROWS]
    scratch += [pltpu.VMEM((FINE.rows, chans, LANES), BF16), pltpu.VMEM((chans, TILE * TILE), F32)]
    scratch += [pltpu.SemaphoreType.DMA((9,)), pltpu.SemaphoreType.DMA((8, ways))]
    out = pl.pallas_call(
        functools.partial(step_kernel, tiles, ways),
        out_shape=jax.ShapeDtypeStruct(features.shape[1:], BF16),
        in_specs=[VMEM_SPEC] * 15,
        out_specs=VMEM_SPEC,
        scratch_shapes=scratch,
        compiler_params=pltpu.CompilerParams(
            collective_id=0, has_side_effects=True, vmem_limit_bytes=48 * 1024 * 1024
        ),
        name="ocean_step",
    )(
        wet_slots[None],
        device_of[None],
        features[0],
        land_mask,
        depth_weight,
        depth_bias,
        norm_gain,
        norm_bias,
        up_weight,
        up_bias,
        down_weight,
        down_bias,
        layer_scale,
        pool_weight.T,
        spread_weight.T,
    )
    return out[None]


def solution(mesh):
    placed = (
        P("tile", "chan", None),
        P("tile", None),
        P(),
        P(),
        P(None, "chan", None),
        P(None, "chan"),
        P(),
        P(),
        P(),
        P(),
        P(),
        P(),
        P(None, "chan"),
        P("chan", None),
        P("chan", None),
    )
    return jax.shard_map(
        functools.partial(per_device, mesh.shape["chan"]),
        mesh=mesh,
        in_specs=placed,
        out_specs=P("tile", "chan", None),
        check_vma=False,
    )
```

time: 91.5 us -> 74.8 us (0.82)
  local copies, waits for them, and re-layouts: 8.13 us -> 2.14 us
  Pallas kernels: 77.2 us -> 72.2 us
  other arithmetic: 4.43 us -> 0 us
    pallas_call x1, Pallas kernels: 77.2 us -> 72.2 us  [per_device(): pl.pallas_call(functools.partial(step_kernel, tiles, ways), out_shape=jax...]
    unnamed x37 -> x30, local copies, waits for them, and re-layouts: 5.94 us -> 2.14 us
    reduce_sum x2 -> x0, other arithmetic: 2.5 us -> none  [the longest x1 2.39 us: source_table(): jnp.sum(jnp.where(source_slot[:, :, None] == wet_slots[None, None, :], de...]
    concatenate x3 -> x0, other arithmetic: 1.26 us -> none  [the longest x2 1.19 us: source_table(): return jnp.concatenate([table, at_fold], axis=1)]
where the time goes in v2:
time: 74.8 us; the launch traced here: 74.5 us
  Pallas kernels  72.2 us (97%)
  local copies, waits for them, and re-layouts  2.14 us (3%)
    pallas_call x1, Pallas kernels, per_device(): pl.pallas_call(functools.partial(step_kernel, tiles, ways), out_shape=jax...  72.2 us
    unnamed x30, local copies, waits for them, and re-layouts  2.14 us

profile of v2, /device:TPU:1, one launch (start us, length us, event | category | flops | bytes accessed | tf_op | source)
XLA Modules:
  0.0 74.5 jit_solution(2552901248923541858)
XLA Ops:
  0.0 0.0 copy-start.3
  0.0 0.0 copy-start.4
  0.0 0.0 copy-start.5
  0.0 0.0 copy-start.6
  0.0 0.0 copy-start.7
  0.1 0.0 copy-start.8
  0.1 0.0 copy-start.9
  0.1 1.4 %copy.16.up_ref = bf16[2,768,192]{2,1,0:T(8,128)(2,1)S(1)} copy(bf16[2,768,192]{1,2,0:T(8,128)(2,1)} %param.23) | data formatting | bytes 1179648 | tf_op args[8]
  1.5 0.0 copy-done
  1.5 0.0 copy-done.1
  1.5 0.0 copy-done.2
  1.5 0.0 copy-done.3
  1.6 0.0 copy-done.4
  1.6 0.0 copy-done.5
  1.6 0.0 copy-done.6
  1.6 0.0 copy-done.7
  1.6 0.0 copy-done.8
  1.6 0.0 copy-done.9
  1.6 0.0 copy-done.10
  1.6 0.0 copy-done.11
  1.6 0.0 copy-done.12
  1.6 0.0 copy-done.13
  1.7 72.2 %ocean_step.1 = bf16[48,2304]{1,0:T(8,128)(2,1)S(1)} custom-call(s32[1,128]{1,0:T(1,128)S(1)} %bitcast.10, s32[1,128]{1,0:T(1,128)S(1)} %bitcast.11, bf16[48,2304]{1,0:T(8,128)(2,1)S(1)} %bitcast.7, s32[1,2304]{1,0:T(1,128)S(1)} %copy-done.3, f32[2,48,49]{2,1,0:T(8,128)S(1)} %copy-done.2, f32[2,48]{1,0:T(2,128)S(1)} %copy-done.10, f32[2,192]{1,0:T(2,128)S(1)} %copy-done.5, ...), custom_call_target="tpu_custom_call" | custom-call | tf_op jit(solution)/shard_map/ocean_step/pallas_call | solution.py:555
  73.8 0.7 copy.18
  (7 shorter events, 0.0 us)
Async XLA Ops:
  0.0 1.5 %copy-start = (bf16[2,192,768]{2,1,0:T(8,128)(2,1)S(1)}, bf16[2,192,768]{2,1,0:T(8,128)(2,1)}, u32[]{:S(2)}) copy-start(bf16[2,192,768]{2,1,0:T(8,128)(2,1)} %down_ref.1) | copy-start | bytes 1769476
  0.0 1.5 %copy-start.1 = (bf16[1,48,2304]{2,1,0:T(8,128)(2,1)S(1)}, bf16[1,48,2304]{2,1,0:T(8,128)(2,1)}, u32[]{:S(2)}) copy-start(bf16[1,48,2304]{2,1,0:T(8,128)(2,1)} %param.15) | copy-start | bytes 663556
  0.0 1.5 %copy-start.2 = (f32[2,48,49]{2,1,0:T(8,128)S(1)}, f32[2,48,49]{2,1,0:T(8,128)}, u32[]{:S(2)}) copy-start(f32[2,48,49]{2,1,0:T(8,128)} %taps_ref.1) | copy-start | bytes 56452
  0.0 1.5 %copy-start.3 = (s32[1,2304]{1,0:T(1,128)S(1)}, s32[1,2304]{1,0:T(1,128)}, u32[]{:S(2)}) copy-start(s32[1,2304]{1,0:T(1,128)} %land_ref.1) | copy-start | bytes 27652
  0.0 1.5 %copy-start.4 = (f32[2,768]{1,0:T(2,128)S(1)}, f32[2,768]{1,0:T(2,128)}, u32[]{:S(2)}) copy-start(f32[2,768]{1,0:T(2,128)} %up_bias_ref.1) | copy-start | bytes 18436
  0.0 1.5 %copy-start.5 = (f32[2,192]{1,0:T(2,128)S(1)}, f32[2,192]{1,0:T(2,128)}, u32[]{:S(2)}) copy-start(f32[2,192]{1,0:T(2,128)} %gain_ref.1) | copy-start | bytes 4612
  0.0 1.5 %copy-start.6 = (f32[2,192]{1,0:T(2,128)S(1)}, f32[2,192]{1,0:T(2,128)}, u32[]{:S(2)}) copy-start(f32[2,192]{1,0:T(2,128)} %shift_ref.1) | copy-start | bytes 4612
  0.0 1.5 %copy-start.7 = (f32[2,192]{1,0:T(2,128)S(1)}, f32[2,192]{1,0:T(2,128)}, u32[]{:S(2)}) copy-start(f32[2,192]{1,0:T(2,128)} %down_bias_ref.1) | copy-start | bytes 4612
  0.1 1.5 %copy-start.8 = (f32[48,4]{0,1:T(4,128)S(1)}, f32[48,4]{0,1:T(4,128)}, u32[]{:S(2)}) copy-start(f32[48,4]{0,1:T(4,128)} %param.28) | copy-start | bytes 2308
  0.1 1.5 %copy-start.9 = (f32[48,4]{0,1:T(4,128)S(1)}, f32[48,4]{0,1:T(4,128)}, u32[]{:S(2)}) copy-start(f32[48,4]{0,1:T(4,128)} %param.29) | copy-start | bytes 2308
  0.1 1.5 %copy-start.10 = (f32[2,48]{1,0:T(2,128)S(1)}, f32[2,48]{1,0:T(2,128)}, u32[]{:S(2)}) copy-start(f32[2,48]{1,0:T(2,128)} %bias_ref.1) | copy-start | bytes 1156
  0.1 1.5 %copy-start.11 = (f32[2,48]{1,0:T(2,128)S(1)}, f32[2,48]{1,0:T(2,128)}, u32[]{:S(2)}) copy-start(f32[2,48]{1,0:T(2,128)} %scale_ref.1) | copy-start | bytes 1156
  0.1 1.5 %copy-start.12 = (s32[128]{0:T(128)S(1)}, s32[128]{0:T(128)}, u32[]{:S(2)}) copy-start(s32[128]{0:T(128)} %param.17) | copy-start | bytes 1540
  0.1 1.5 %copy-start.13 = (s32[128]{0:T(128)S(1)}, s32[128]{0:T(128)}, u32[]{:S(2)}) copy-start(s32[128]{0:T(128)} %param.18) | copy-start | bytes 1540

commit v3 on v2

--- a/solution.py
+++ b/solution.py
@@ -32,7 +32,6 @@
 
 FINE = Level(TILE, 2, 8)
 COARSE = Level(TILE // 2, 4, 3)
-MIX_ROWS = (6, 2)
 
 
 def roll(x, shift):
@@ -70,6 +69,37 @@
     return fold
 
 
+def each_other_tile(me, tiles, body):
+    layer = 16
+    deep = tiles // layer
+    mine = me // layer
+    low = lax.rem(me, layer)
+
+    @pl.loop(0, deep - 1)
+    def _(n):
+        half = (n + 1) // 2
+        z = lax.rem(mine + deep // 2 + half * (2 * lax.rem(n, 2) - 1) + deep, deep)
+
+        @pl.loop(0, layer // 4)
+        def _(i):
+            body([z * layer + lax.rem(low + layer // 2 + 4 * i + t, layer) for t in range(4)])
+
+    @pl.loop(0, layer // 4 - 1)
+    def _(i):
+        body([mine * layer + lax.rem(low + 4 + 4 * i + t, layer) for t in range(4)])
+
+    body([mine * layer + lax.rem(low + t, layer) for t in range(1, 4)])
+
+
+def each_piece(me, pieces, tiles, body):
+    start = (me * pieces) // tiles + pieces // 2
+
+    @pl.loop(0, pieces // 2)
+    def _(i):
+        body(lax.rem(start + i, pieces))
+        body(lax.rem(start + pieces - 1 - i, pieces))
+
+
 def lane_ids(shape=(1, LANES)):
     return lax.broadcasted_iota(jnp.int32, shape, len(shape) - 1)
 
@@ -116,8 +146,7 @@
     pieces = outgoing.shape[0]
     units = level.units
 
-    @pl.loop(0, pieces)
-    def _(p):
+    def send(p):
         target = (p * tiles) // pieces
 
         @pl.when(target != me)
@@ -131,25 +160,25 @@
                 device_id_type=MESH,
             ).start()
 
-
-def route(level, tiles, table_ref, outgoing, held, picked, got, send_a, recv_a, send_b, recv_b):
+    each_piece(me, pieces, tiles, send)
+
+
+def serve_strips(level, tiles, table_ref, outgoing, held, picked, got, recv_a, send_b, recv_b):
     me = lax.axis_index("tile")
     pieces = outgoing.shape[0]
     piece = (me * pieces + tiles - 1) // tiles
     holds = jnp.logical_and(piece < pieces, (piece * tiles) // pieces == me)
     units, edge = level.units, level.edge_units
 
-    def send(target, k):
-        @pl.when(k > 0)
-        def _():
-            pltpu.make_async_remote_copy(
-                src_ref=picked.at[target],
-                dst_ref=got.at[piece],
-                send_sem=send_b,
-                recv_sem=recv_b,
-                device_id={"tile": target},
-                device_id_type=MESH,
-            ).start()
+    def send(target):
+        pltpu.make_async_remote_copy(
+            src_ref=picked.at[target],
+            dst_ref=got.at[piece],
+            send_sem=send_b,
+            recv_sem=recv_b,
+            device_id={"tile": target},
+            device_id_type=MESH,
+        ).start()
 
     @pl.when(holds)
     def _():
@@ -164,9 +193,7 @@
 
         @pl.when(lax.rem(piece, 2) == 0)
         def _():
-            @pl.loop(0, tiles)
-            def _(k):
-                target = lax.rem(me + k, tiles)
+            def pick(target):
                 below = [table_ref[target, band] * units + edge for band in range(3)]
                 fold = table_ref[target, 8] * edge
                 above = [table_ref[target, band] * units + fold for band in range(5, 8)]
@@ -177,22 +204,45 @@
                         right = held[base[2] + unit].astype(F32)
                         row = jnp.where(left_lanes, left, jnp.where(own_lanes, own, right))
                         picked[target, place] = row.astype(BF16)
-                send(target, k)
+
+            def pick_and_send(targets):
+                for target in targets:
+                    pick(target)
+                for target in targets:
+                    send(target)
+
+            each_other_tile(me, tiles, pick_and_send)
+            pick(me)
 
         @pl.when(lax.rem(piece, 2) == 1)
         def _():
-            @pl.loop(0, tiles)
-            def _(k):
-                target = lax.rem(me + k, tiles)
+            def pick(target):
                 at_left = table_ref[target, 3] * units
                 at_right = table_ref[target, 4] * units
                 for unit in range(level.side_units):
                     left = held[at_left + unit].astype(F32)
                     right = held[at_right + unit].astype(F32)
                     picked[target, unit] = jnp.where(first_lanes, right, left).astype(BF16)
-                send(target, k)
+
+            def pick_and_send(targets):
+                for target in targets:
+                    pick(target)
+                for target in targets:
+                    send(target)
+
+            each_other_tile(me, tiles, pick_and_send)
+            pick(me)
 
         got[piece] = picked[me]
+
+def collect_strips(tiles, outgoing, picked, got, send_a, send_b, recv_b):
+    me = lax.axis_index("tile")
+    pieces = outgoing.shape[0]
+    piece = (me * pieces + tiles - 1) // tiles
+    holds = jnp.logical_and(piece < pieces, (piece * tiles) // pieces == me)
+
+    @pl.when(holds)
+    def _():
         others = outgoing.at[pl.ds(0, pieces - 1)]
         pltpu.make_async_copy(others, others, send_a).wait()
         arrived = got.at[pl.ds(0, pieces - 1)]
@@ -206,7 +256,15 @@
         pltpu.make_async_copy(got, got, recv_b).wait()
 
 
-def set_halo(level, grid, units, got, fold):
+def close_parts(level, grid):
+    lane = lane_ids()
+    rows, pitch = level.rows, level.pitch
+    for k in range(3):
+        grid[k] = jnp.where(lane < pitch, 0.0, roll(grid[rows + k], pitch))
+        grid[rows + 3 + k] = jnp.where(lane >= LANES - pitch, 0.0, roll(grid[3 + k], -pitch))
+
+
+def set_rim(level, rim, units, got, fold):
     for role in range(2):
         for unit in range((2 * level.edge_units, level.side_units)[role]):
             for p in range(got.shape[0] // 2):
@@ -220,8 +278,8 @@
             j = unit * level.slots + slot
             if j >= rows:
                 continue
-            own = jnp.where(q < 3, roll(value, -6 * slot - 3), grid[3 + j])
-            grid[3 + j] = jnp.where(q < side + 3, own, roll(value, side + 3 - 6 * slot))
+            own = jnp.where(q < 3, roll(value, -6 * slot - 3), 0.0)
+            rim[3 + j] = jnp.where(q < side + 3, own, roll(value, side + 3 - 6 * slot))
     backwards = (
         lax.broadcasted_iota(jnp.int32, (LANES, LANES), 0) + lax.broadcasted_iota(jnp.int32, (LANES, LANES), 1)
         == side + 5
@@ -230,14 +288,14 @@
     mirrored = []
     for k in range(3):
         below = roll(units[0, k // level.parts].astype(F32), -(k % level.parts) * pitch)
-        grid[k] = jnp.where(lane < pitch, below, roll(grid[rows + k], pitch))
+        rim[k] = jnp.where(lane < pitch, below, roll(rim[rows + k], pitch))
         row = roll(units[0, edge + k // level.parts].astype(F32), -(k % level.parts) * pitch)
         above.append(row)
         mirrored.append(jnp.dot(row.astype(BF16), backwards, preferred_element_type=F32))
     for k in range(3):
         top = jnp.where(fold > 0.5, mirrored[2 - k], above[k])
         top = roll(top, LANES - pitch)
-        grid[rows + 3 + k] = jnp.where(lane >= LANES - pitch, top, roll(grid[3 + k], -pitch))
+        rim[rows + 3 + k] = jnp.where(lane >= LANES - pitch, top, roll(rim[3 + k], -pitch))
 
 
 def start_swap(ways, source, target, send, recv, window):
@@ -263,38 +321,96 @@
         pltpu.make_async_copy(block, block, recv.at[k]).wait()
 
 
-def depthwise(level, lev, grid, taps_ref, cols, conv, sent, every, send, recv):
+def start_gather(ways, source, target, send, recv, window):
+    me = lax.axis_index("chan")
+    for k in range(1, ways):
+        pltpu.make_async_remote_copy(
+            src_ref=source.at[window],
+            dst_ref=target.at[(me,) + window],
+            send_sem=send.at[k],
+            recv_sem=recv.at[k],
+            device_id={"chan": lax.rem(me + k, ways)},
+            device_id_type=MESH,
+        ).start()
+
+
+def finish_gather(ways, source, target, send, recv):
+    target[lax.axis_index("chan")] = source[...]
+    for k in range(1, ways):
+        pltpu.make_async_copy(source, source, send.at[k]).wait()
+        pltpu.make_async_copy(source, source, recv.at[k]).wait()
+
+
+def depthwise_inside(level, lev, grid, taps_ref, cols, conv):
     rows = level.rows
-    ways, per = sent.shape[:2]
+
+    @pl.loop(0, grid.shape[1] // 8)
+    def _(g):
+        at = pl.ds(pl.multiple_of(g * 8, 8), 8)
+        taps = taps_ref[lev, at, :]
+        total = [jnp.broadcast_to(cols[at, lev : lev + 1], (8, LANES))] * rows
+        for b in range(7):
+            weights = [jnp.broadcast_to(taps[:, 7 * a + b : 7 * a + b + 1], (8, LANES)) for a in range(7)]
+            for j in range(rows + 6):
+                shifted = roll(grid[j, at, :], -b)
+                for a in range(7):
+                    if 0 <= j - a < rows:
+                        total[j - a] = total[j - a] + weights[a] * shifted
+        for j in range(rows):
+            conv[j, at, :] = total[j]
+
+
+def depthwise_rim(level, lev, ways, rim, taps_ref, conv, sent, every, send, recv):
+    rows = level.rows
+    split = len(sent.shape) == 4
+    per = sent.shape[1] if split else rows
     wide = 16
-    for j in range(rows, ways * per):
-        sent[j // per, j % per] = jnp.zeros(sent.shape[2:], BF16)
-
-    @pl.loop(0, grid.shape[1] // wide)
+    near = lax.rem(lane_ids((8, LANES)), level.pitch) < 8
+
+    @pl.loop(0, rim.shape[1] // wide)
     def _(g):
         both = pl.ds(pl.multiple_of(g * wide, wide), wide)
         for part in range(2):
             at = pl.ds(pl.multiple_of(g * wide + part * 8, 8), 8)
             taps = taps_ref[lev, at, :]
-            total = [jnp.broadcast_to(cols[at, lev : lev + 1], (8, LANES))] * rows
+            total = [conv[j, at, :] for j in range(rows)]
+
+            def tap(a, b):
+                return jnp.broadcast_to(taps[:, 7 * a + b : 7 * a + b + 1], (8, LANES))
+
             for b in range(7):
-                weights = [jnp.broadcast_to(taps[:, 7 * a + b : 7 * a + b + 1], (8, LANES)) for a in range(7)]
-                for j in range(rows + 6):
-                    shifted = roll(grid[j, at, :], -b)
+                weights = [tap(a, b) for a in range(7)]
+                for j in (0, 1, 2, rows + 3, rows + 4, rows + 5):
+                    shifted = roll(rim[j, at, :], -b)
+                    for a in range(7):
+                        if 0 <= j - a < rows:
+                            total[j - a] = total[j - a] + weights[a] * shifted
+            for b in range(3):
+                weights = [jnp.where(near, tap(a, b), tap(a, b + 4)) for a in range(7)]
+                for j in range(3, rows + 3):
+                    cells = rim[j, at, :]
+                    shifted = jnp.where(near, roll(cells, -b), roll(cells, -b - 4))
                     for a in range(7):
                         if 0 <= j - a < rows:
                             total[j - a] = total[j - a] + weights[a] * shifted
             for j in range(rows):
                 conv[j, at, :] = total[j]
         for j in range(rows):
-            sent[j // per, j % per, both, :] = conv[j, both, :].astype(BF16)
-        start_swap(ways, sent, every, send, recv, (slice(None), both))
-
-    finish_swap(ways, sent, every, send, recv)
-
-
-def mix(lev, every, tall_ref, up_ref, upb_ref, down_ref, branch, back, send, recv):
+            at = (j // per, j % per) if split else (j,)
+            sent[at + (both, slice(None))] = conv[j, both, :].astype(BF16)
+        start = start_swap if split else start_gather
+        start(ways, sent, every, send, recv, (slice(None), both))
+
+    finish = finish_swap if split else finish_gather
+    finish(ways, sent, every, send, recv)
+
+
+def mix(lev, every, tall_ref, up_ref, upb_ref, down_ref, branch, back=None, send=None, recv=None):
     ways, count, chans, _ = every.shape
+    own_count = ways * chans if back is not None else chans
+    own = slice(None)
+    if back is None:
+        own = pl.ds(pl.multiple_of(lax.axis_index("chan") * chans, chans), chans)
     hidden_size = up_ref.shape[1]
     step = 256
 
@@ -309,18 +425,23 @@
             scaled = centred * lax.rsqrt(spread + norm_eps)
             sides.append((scaled * tall_ref[:, lev : lev + 1] + tall_ref[:, 2 + lev : 3 + lev]).astype(BF16))
         normed = jnp.concatenate(sides, axis=1)
-        total = jnp.broadcast_to(tall_ref[:, 4 + lev : 5 + lev], (ways * chans, 2 * LANES))
+        total = jnp.broadcast_to(tall_ref[own, 4 + lev : 5 + lev], (own_count, 2 * LANES))
         for h in range(hidden_size // step):
             at = slice(h * step, (h + 1) * step)
             hidden = jnp.dot(up_ref[lev, at, :], normed, preferred_element_type=F32) + upb_ref[at, lev : lev + 1]
             hidden = 0.5 * hidden * (1.0 + lax.erf(hidden * (0.5**0.5)))
-            total = total + jnp.dot(down_ref[lev, :, at], hidden.astype(BF16), preferred_element_type=F32)
+            total = total + jnp.dot(down_ref[lev, own, at], hidden.astype(BF16), preferred_element_type=F32)
         for jj in range(2):
             half = total[:, jj * LANES : (jj + 1) * LANES]
-            branch[:, 2 * i + jj] = half.reshape(ways, chans, LANES).astype(BF16)
-        start_swap(ways, branch, back, send, recv, (pl.ds(2 * i, 2),))
-
-    finish_swap(ways, branch, back, send, recv)
+            if back is None:
+                branch[2 * i + jj] = half
+            else:
+                branch[:, 2 * i + jj] = half.reshape(ways, chans, LANES).astype(BF16)
+        if back is not None:
+            start_swap(ways, branch, back, send, recv, (pl.ds(2 * i, 2),))
+
+    if back is not None:
+        finish_swap(ways, branch, back, send, recv)
 
 
 def columns(block):
@@ -359,6 +480,8 @@
     gather,
     grid0,
     grid1,
+    rim0,
+    rim1,
     units0,
     units1,
     outgoing0,
@@ -377,7 +500,6 @@
     branch0,
     branch1,
     back0,
-    back1,
     fine,
     flat,
     sems,
@@ -393,15 +515,18 @@
 
     @pl.when(holds)
     def _():
-        @pl.loop(1, tiles)
-        def _(k):
-            pl.semaphore_signal(barrier, inc=1, device_id={"tile": lax.rem(me + k, tiles)}, device_id_type=MESH)
+        def greet(targets):
+            for target in targets:
+                pl.semaphore_signal(barrier, inc=1, device_id={"tile": target}, device_id_type=MESH)
+
+        each_other_tile(me, tiles, greet)
 
     @pl.when(jnp.logical_not(holds))
     def _():
-        @pl.loop(0, pieces)
-        def _(p):
+        def greet(p):
             pl.semaphore_signal(barrier, inc=1, device_id={"tile": (p * tiles) // pieces}, device_id_type=MESH)
+
+        each_piece(me, pieces, tiles, greet)
 
     for k in range(1, ways):
         pl.semaphore_signal(barrier, inc=1, device_id={"chan": lax.rem(chan + k, ways)}, device_id_type=MESH)
@@ -430,10 +555,14 @@
     fold = source_table(2 * tiles // GRID_Y, GRID_Y, wet_ref, device_of_ref, table_v)
     table_copy = pltpu.make_async_copy(table_v, table_s, sems.at[8])
     table_copy.start()
+    table_copy.wait()
+    serve_strips(FINE, tiles, table_s, outgoing0, held0, picked0, got0, sems.at[1], sems.at[2], sems.at[3])
     rows_a[...] = jnp.zeros(rows_a.shape, F32)
     for at, ref in ((0, bias_ref), (2, scale_ref), (4, pool_ref), (8, spread_ref)):
         rows_a[at : at + ref.shape[0], :chans] = ref[...]
     cols[...] = columns(rows_a[...])[:chans]
+    close_parts(FINE, grid0)
+    depthwise_inside(FINE, 0, grid0, taps_ref, cols, conv)
     rows_b[...] = jnp.zeros(rows_b.shape, F32)
     for at, ref in ((0, gain_ref), (2, shift_ref), (4, down_bias_ref)):
         rows_b[at : at + 2, : ways * chans] = ref[...]
@@ -460,13 +589,11 @@
             sides.append(jnp.maximum(value, roll(value, -1)).astype(BF16))
         value = jnp.dot(jnp.concatenate(sides, axis=1), gather[...], preferred_element_type=F32)
         mask1[j] = roll(value, -3)[0:1]
-    table_copy.wait()
-
-    route(FINE, tiles, table_s, outgoing0, held0, picked0, got0, sems.at[0], sems.at[1], sems.at[2], sems.at[3])
-    set_halo(FINE, grid0, units0, got0, fold)
-    depthwise(FINE, 0, grid0, taps_ref, cols, conv, sent0, every0, swaps.at[0], swaps.at[1])
+    collect_strips(tiles, outgoing0, picked0, got0, sems.at[0], sems.at[2], sems.at[3])
+    set_rim(FINE, rim0, units0, got0, fold)
+    depthwise_rim(FINE, 0, ways, rim0, taps_ref, conv, sent0, every0, swaps.at[0], swaps.at[1])
     mix(0, every0, tall, up_ref, upb, down_ref, branch0, back0, swaps.at[2], swaps.at[3])
-    per = MIX_ROWS[0]
+    per = sent0.shape[1]
     scale = cols[:, 2:3]
     for j in range(FINE.rows):
         value = roll(grid0[3 + j], -3) + scale * back0[j // per, j % per].astype(F32)
@@ -482,18 +609,20 @@
         grid1[3 + j] = jnp.dot(jnp.concatenate(sides, axis=1), gather[...], preferred_element_type=F32)
     cut_units(COARSE, grid1, units1, outgoing1)
     scatter_strips(COARSE, tiles, outgoing1, held1, sems.at[4], sems.at[5])
-    route(COARSE, tiles, table_s, outgoing1, held1, picked1, got1, sems.at[4], sems.at[5], sems.at[6], sems.at[7])
-    set_halo(COARSE, grid1, units1, got1, fold)
-    depthwise(COARSE, 1, grid1, taps_ref, cols, conv, sent1, every1, swaps.at[4], swaps.at[5])
-    mix(1, every1, tall, up_ref, upb, down_ref, branch1, back1, swaps.at[6], swaps.at[7])
-    per = MIX_ROWS[1]
+    serve_strips(COARSE, tiles, table_s, outgoing1, held1, picked1, got1, sems.at[5], sems.at[6], sems.at[7])
+    close_parts(COARSE, grid1)
+    depthwise_inside(COARSE, 1, grid1, taps_ref, cols, conv)
+    collect_strips(tiles, outgoing1, picked1, got1, sems.at[4], sems.at[6], sems.at[7])
+    set_rim(COARSE, rim1, units1, got1, fold)
+    depthwise_rim(COARSE, 1, ways, rim1, taps_ref, conv, sent1, every1, swaps.at[4], swaps.at[5])
+    mix(1, every1, tall, up_ref, upb, down_ref, branch1)
     scale = cols[:, 3:4]
     source = lax.broadcasted_iota(jnp.int32, (LANES, LANES), 0)
     target = lax.broadcasted_iota(jnp.int32, (LANES, LANES), 1)
     odd = lax.rem(lane, 2) == 1
     spread = [jnp.where(odd, cols[:, 9 + 2 * t : 10 + 2 * t], cols[:, 8 + 2 * t : 9 + 2 * t]) for t in range(2)]
     for j in range(COARSE.rows):
-        value = roll(grid1[3 + j], -3) + scale * back1[j // per, j % per].astype(F32)
+        value = roll(grid1[3 + j], -3) + scale * branch1[j]
         coarse = (mask1[j] * value).astype(BF16)
         for t in range(2):
             wanted = 64 * (target // 64) + 32 * t + lax.rem(target, 64) // 2
@@ -540,16 +669,18 @@
         pltpu.VMEM((FINE.rows, 1, LANES), F32),
         pltpu.VMEM((COARSE.rows, 1, LANES), F32),
         pltpu.VMEM((2 * LANES, LANES), BF16),
-        pltpu.VMEM((FINE.rows + 6, chans, LANES), F32),
-        pltpu.VMEM((COARSE.rows + 6, chans, LANES), F32),
     ]
+    scratch += [pltpu.VMEM((level.rows + 6, chans, LANES), F32) for level in levels] * 2
     scratch += [pltpu.VMEM((2, level.units, chans, LANES), BF16) for level in levels]
     scratch += [pltpu.VMEM((chans, level.units, 2, LANES), BF16) for level in levels]
     scratch += [pltpu.VMEM(((tiles + 1) * level.units, 2, LANES), BF16) for level in levels]
     scratch += [pltpu.VMEM((tiles, level.units, 2, LANES), BF16) for level in levels]
     scratch += [pltpu.VMEM((chans, level.units, 2, LANES), BF16) for level in levels]
     scratch += [pltpu.VMEM((FINE.rows, chans, LANES), F32)]
-    scratch += [pltpu.VMEM((ways, per, chans, LANES), BF16) for _ in range(4) for per in MIX_ROWS]
+    quarter = pltpu.VMEM((ways, FINE.rows // ways, chans, LANES), BF16)
+    scratch += [quarter, pltpu.VMEM((COARSE.rows, chans, LANES), BF16)]
+    scratch += [quarter, pltpu.VMEM((ways, COARSE.rows, chans, LANES), BF16)]
+    scratch += [quarter, pltpu.VMEM((COARSE.rows, chans, LANES), F32), quarter]
     scratch += [pltpu.VMEM((FINE.rows, chans, LANES), BF16), pltpu.VMEM((chans, TILE * TILE), F32)]
     scratch += [pltpu.SemaphoreType.DMA((9,)), pltpu.SemaphoreType.DMA((8, ways))]
     out = pl.pallas_call(

time: 74.8 us -> 73.2 us (0.979)
  Pallas kernels: 72.2 us -> 70.7 us
    pallas_call x1, Pallas kernels: 72.2 us -> 70.7 us  [per_device(): pl.pallas_call(functools.partial(step_kernel, tiles, ways), out_shape=jax...]
where the time goes in v3:
time: 73.2 us; the launch traced here: 73 us
  Pallas kernels  70.7 us (97%)
  local copies, waits for them, and re-layouts  2.14 us (3%)
    pallas_call x1, Pallas kernels, per_device(): pl.pallas_call(functools.partial(step_kernel, tiles, ways), out_shape=jax...  70.7 us
    unnamed x30, local copies, waits for them, and re-layouts  2.14 us

profile of v3, /device:TPU:1, one launch (start us, length us, event | category | flops | bytes accessed | tf_op | source)
XLA Modules:
  0.0 73.0 jit_solution(15441162735492911158)
XLA Ops:
  0.0 0.0 copy-start.3
  0.0 0.0 copy-start.4
  0.0 0.0 copy-start.5
  0.0 0.0 copy-start.6
  0.0 0.0 copy-start.7
  0.1 0.0 copy-start.8
  0.1 0.0 copy-start.9
  0.1 0.0 copy-start.10
  0.1 0.0 copy-start.11
  0.1 0.0 copy-start.12
  0.1 0.0 copy-start.13
  0.1 1.4 %copy.16.up_ref = bf16[2,768,192]{2,1,0:T(8,128)(2,1)S(1)} copy(bf16[2,768,192]{1,2,0:T(8,128)(2,1)} %param.23) | data formatting | bytes 1179648 | tf_op args[8]
  1.5 0.0 copy-done
  1.5 0.0 copy-done.1
  1.5 0.0 copy-done.2
  1.5 0.0 copy-done.3
  1.6 0.0 copy-done.4
  1.6 0.0 copy-done.5
  1.6 0.0 copy-done.6
  1.6 0.0 copy-done.7
  1.6 0.0 copy-done.8
  1.6 0.0 copy-done.9
  1.7 70.7 %ocean_step.1 = bf16[48,2304]{1,0:T(8,128)(2,1)S(1)} custom-call(s32[1,128]{1,0:T(1,128)S(1)} %bitcast.10, s32[1,128]{1,0:T(1,128)S(1)} %bitcast.11, bf16[48,2304]{1,0:T(8,128)(2,1)S(1)} %bitcast.7, s32[1,2304]{1,0:T(1,128)S(1)} %copy-done.3, f32[2,48,49]{2,1,0:T(8,128)S(1)} %copy-done.2, f32[2,48]{1,0:T(2,128)S(1)} %copy-done.10, f32[2,192]{1,0:T(2,128)S(1)} %copy-done.5, ...), custom_call_target="tpu_custom_call" | custom-call | tf_op jit(solution)/shard_map/ocean_step/pallas_call | solution.py:686
  72.3 0.7 copy.18
  (7 shorter events, 0.0 us)
Async XLA Ops:
  0.0 1.5 %copy-start = (bf16[2,192,768]{2,1,0:T(8,128)(2,1)S(1)}, bf16[2,192,768]{2,1,0:T(8,128)(2,1)}, u32[]{:S(2)}) copy-start(bf16[2,192,768]{2,1,0:T(8,128)(2,1)} %down_ref.1) | copy-start | bytes 1769476
  0.0 1.5 %copy-start.1 = (bf16[1,48,2304]{2,1,0:T(8,128)(2,1)S(1)}, bf16[1,48,2304]{2,1,0:T(8,128)(2,1)}, u32[]{:S(2)}) copy-start(bf16[1,48,2304]{2,1,0:T(8,128)(2,1)} %param.15) | copy-start | bytes 663556
  0.0 1.5 %copy-start.2 = (f32[2,48,49]{2,1,0:T(8,128)S(1)}, f32[2,48,49]{2,1,0:T(8,128)}, u32[]{:S(2)}) copy-start(f32[2,48,49]{2,1,0:T(8,128)} %taps_ref.1) | copy-start | bytes 56452
  0.0 1.5 %copy-start.3 = (s32[1,2304]{1,0:T(1,128)S(1)}, s32[1,2304]{1,0:T(1,128)}, u32[]{:S(2)}) copy-start(s32[1,2304]{1,0:T(1,128)} %land_ref.1) | copy-start | bytes 27652
  0.0 1.5 %copy-start.4 = (f32[2,768]{1,0:T(2,128)S(1)}, f32[2,768]{1,0:T(2,128)}, u32[]{:S(2)}) copy-start(f32[2,768]{1,0:T(2,128)} %up_bias_ref.1) | copy-start | bytes 18436
  0.0 1.5 %copy-start.5 = (f32[2,192]{1,0:T(2,128)S(1)}, f32[2,192]{1,0:T(2,128)}, u32[]{:S(2)}) copy-start(f32[2,192]{1,0:T(2,128)} %gain_ref.1) | copy-start | bytes 4612
  0.0 1.5 %copy-start.6 = (f32[2,192]{1,0:T(2,128)S(1)}, f32[2,192]{1,0:T(2,128)}, u32[]{:S(2)}) copy-start(f32[2,192]{1,0:T(2,128)} %shift_ref.1) | copy-start | bytes 4612
  0.0 1.5 %copy-start.7 = (f32[2,192]{1,0:T(2,128)S(1)}, f32[2,192]{1,0:T(2,128)}, u32[]{:S(2)}) copy-start(f32[2,192]{1,0:T(2,128)} %down_bias_ref.1) | copy-start | bytes 4612
  0.1 1.5 %copy-start.8 = (f32[48,4]{0,1:T(4,128)S(1)}, f32[48,4]{0,1:T(4,128)}, u32[]{:S(2)}) copy-start(f32[48,4]{0,1:T(4,128)} %param.28) | copy-start | bytes 2308
  0.1 1.5 %copy-start.9 = (f32[48,4]{0,1:T(4,128)S(1)}, f32[48,4]{0,1:T(4,128)}, u32[]{:S(2)}) copy-start(f32[48,4]{0,1:T(4,128)} %param.29) | copy-start | bytes 2308
  0.1 1.5 %copy-start.10 = (f32[2,48]{1,0:T(2,128)S(1)}, f32[2,48]{1,0:T(2,128)}, u32[]{:S(2)}) copy-start(f32[2,48]{1,0:T(2,128)} %bias_ref.1) | copy-start | bytes 1156
  0.1 1.5 %copy-start.11 = (f32[2,48]{1,0:T(2,128)S(1)}, f32[2,48]{1,0:T(2,128)}, u32[]{:S(2)}) copy-start(f32[2,48]{1,0:T(2,128)} %scale_ref.1) | copy-start | bytes 1156
  0.1 1.5 %copy-start.12 = (s32[128]{0:T(128)S(1)}, s32[128]{0:T(128)}, u32[]{:S(2)}) copy-start(s32[128]{0:T(128)} %param.17) | copy-start | bytes 1540
  0.1 1.5 %copy-start.13 = (s32[128]{0:T(128)S(1)}, s32[128]{0:T(128)}, u32[]{:S(2)}) copy-start(s32[128]{0:T(128)} %param.18) | copy-start | bytes 1540

commit v4 on v3

--- a/solution.py
+++ b/solution.py
@@ -139,6 +139,9 @@
         for unit in range((2 * level.edge_units, level.side_units)[role]):
             for p in range(outgoing.shape[0] // 2):
                 outgoing[2 * p + role, unit] = units[role, unit, 2 * p : 2 * p + 2, :]
+        for unit in range((2 * level.edge_units, level.side_units)[role], level.units):
+            for p in range(outgoing.shape[0] // 2):
+                outgoing[2 * p + role, unit] = jnp.zeros((2, LANES), BF16)
 
 
 def scatter_strips(level, tiles, outgoing, held, send_a, recv_a):
@@ -298,9 +301,13 @@
         rim[rows + 3 + k] = jnp.where(lane >= LANES - pitch, top, roll(rim[3 + k], -pitch))
 
 
+def peers(ways):
+    return sorted(range(1, ways), key=lambda k: -min(k, ways - k))
+
+
 def start_swap(ways, source, target, send, recv, window):
     me = lax.axis_index("chan")
-    for k in range(1, ways):
+    for k in peers(ways):
         peer = lax.rem(me + k, ways)
         pltpu.make_async_remote_copy(
             src_ref=source.at[(peer,) + window],
@@ -323,7 +330,7 @@
 
 def start_gather(ways, source, target, send, recv, window):
     me = lax.axis_index("chan")
-    for k in range(1, ways):
+    for k in peers(ways):
         pltpu.make_async_remote_copy(
             src_ref=source.at[window],
             dst_ref=target.at[(me,) + window],
@@ -478,6 +485,7 @@
     mask,
     mask1,
     gather,
+    scatter,
     grid0,
     grid1,
     rim0,
@@ -538,8 +546,6 @@
         grid0[3 + j] = jnp.zeros(grid0.shape[1:], F32)
         grid0[3 + j, :, 3 : 3 + TILE] = flat[:, TILE * j : TILE * (j + 1)]
         grid0[3 + j, :, 67 : 67 + TILE] = flat[:, half + TILE * j : half + TILE * (j + 1)]
-    for outgoing in (outgoing0, outgoing1):
-        outgoing[...] = jnp.zeros(outgoing.shape, BF16)
     cut_units(FINE, grid0, units0, outgoing0)
 
     @pl.when(holds)
@@ -612,22 +618,23 @@
     serve_strips(COARSE, tiles, table_s, outgoing1, held1, picked1, got1, sems.at[5], sems.at[6], sems.at[7])
     close_parts(COARSE, grid1)
     depthwise_inside(COARSE, 1, grid1, taps_ref, cols, conv)
+    source = lax.broadcasted_iota(jnp.int32, (LANES, LANES), 0)
+    target = lax.broadcasted_iota(jnp.int32, (LANES, LANES), 1)
+    for t in range(2):
+        wanted = 64 * (target // 64) + 32 * t + lax.rem(target, 64) // 2
+        scatter[t] = jnp.logical_and(source == wanted, lax.rem(target, 64) < TILE).astype(BF16)
     collect_strips(tiles, outgoing1, picked1, got1, sems.at[4], sems.at[6], sems.at[7])
     set_rim(COARSE, rim1, units1, got1, fold)
     depthwise_rim(COARSE, 1, ways, rim1, taps_ref, conv, sent1, every1, swaps.at[4], swaps.at[5])
     mix(1, every1, tall, up_ref, upb, down_ref, branch1)
     scale = cols[:, 3:4]
-    source = lax.broadcasted_iota(jnp.int32, (LANES, LANES), 0)
-    target = lax.broadcasted_iota(jnp.int32, (LANES, LANES), 1)
     odd = lax.rem(lane, 2) == 1
     spread = [jnp.where(odd, cols[:, 9 + 2 * t : 10 + 2 * t], cols[:, 8 + 2 * t : 9 + 2 * t]) for t in range(2)]
     for j in range(COARSE.rows):
         value = roll(grid1[3 + j], -3) + scale * branch1[j]
         coarse = (mask1[j] * value).astype(BF16)
         for t in range(2):
-            wanted = 64 * (target // 64) + 32 * t + lax.rem(target, 64) // 2
-            scatter = jnp.logical_and(source == wanted, lax.rem(target, 64) < TILE).astype(BF16)
-            wide = jnp.dot(coarse, scatter, preferred_element_type=F32)
+            wide = jnp.dot(coarse, scatter[t], preferred_element_type=F32)
             for row in range(2):
                 at = 2 * (j + COARSE.rows * t) + row
                 value = mask[at] * (fine[at].astype(F32) + spread[row] * wide)
@@ -669,6 +676,7 @@
         pltpu.VMEM((FINE.rows, 1, LANES), F32),
         pltpu.VMEM((COARSE.rows, 1, LANES), F32),
         pltpu.VMEM((2 * LANES, LANES), BF16),
+        pltpu.VMEM((2, LANES, LANES), BF16),
     ]
     scratch += [pltpu.VMEM((level.rows + 6, chans, LANES), F32) for level in levels] * 2
     scratch += [pltpu.VMEM((2, level.units, chans, LANES), BF16) for level in levels]

time: 73.2 us -> 72.7 us (level)
  no operation moved by 1% of the time
where the time goes in v4:
time: 72.7 us; the launch traced here: 72.6 us
  Pallas kernels  70.2 us (97%)
  local copies, waits for them, and re-layouts  2.14 us (3%)
    pallas_call x1, Pallas kernels, per_device(): pl.pallas_call(functools.partial(step_kernel, tiles, ways), out_shape=jax...  70.2 us
    unnamed x30, local copies, waits for them, and re-layouts  2.14 us

profile of v4, /device:TPU:1, one launch (start us, length us, event | category | flops | bytes accessed | tf_op | source)
XLA Modules:
  0.0 72.6 jit_solution(6832491766825543518)
XLA Ops:
  0.0 0.0 copy-start.3
  0.0 0.0 copy-start.4
  0.0 0.0 copy-start.5
  0.0 0.0 copy-start.6
  0.0 0.0 copy-start.7
  0.1 0.0 copy-start.8
  0.1 0.0 copy-start.9
  0.1 0.0 copy-start.10
  0.1 0.0 copy-start.11
  0.1 0.0 copy-start.12
  0.1 0.0 copy-start.13
  0.1 1.4 %copy.16.up_ref = bf16[2,768,192]{2,1,0:T(8,128)(2,1)S(1)} copy(bf16[2,768,192]{1,2,0:T(8,128)(2,1)} %param.23) | data formatting | bytes 1179648 | tf_op args[8]
  1.5 0.0 copy-done
  1.5 0.0 copy-done.1
  1.5 0.0 copy-done.2
  1.5 0.0 copy-done.3
  1.6 0.0 copy-done.4
  1.6 0.0 copy-done.5
  1.6 0.0 copy-done.6
  1.6 0.0 copy-done.7
  1.6 0.0 copy-done.8
  1.6 0.0 copy-done.9
  1.7 70.2 %ocean_step.1 = bf16[48,2304]{1,0:T(8,128)(2,1)S(1)} custom-call(s32[1,128]{1,0:T(1,128)S(1)} %bitcast.10, s32[1,128]{1,0:T(1,128)S(1)} %bitcast.11, bf16[48,2304]{1,0:T(8,128)(2,1)S(1)} %bitcast.7, s32[1,2304]{1,0:T(1,128)S(1)} %copy-done.3, f32[2,48,49]{2,1,0:T(8,128)S(1)} %copy-done.2, f32[2,48]{1,0:T(2,128)S(1)} %copy-done.10, f32[2,192]{1,0:T(2,128)S(1)} %copy-done.5, ...), custom_call_target="tpu_custom_call" | custom-call | tf_op jit(solution)/shard_map/ocean_step/pallas_call | solution.py:694
  71.9 0.7 copy.18
  (7 shorter events, 0.0 us)
Async XLA Ops:
  0.0 1.5 %copy-start = (bf16[2,192,768]{2,1,0:T(8,128)(2,1)S(1)}, bf16[2,192,768]{2,1,0:T(8,128)(2,1)}, u32[]{:S(2)}) copy-start(bf16[2,192,768]{2,1,0:T(8,128)(2,1)} %down_ref.1) | copy-start | bytes 1769476
  0.0 1.5 %copy-start.1 = (bf16[1,48,2304]{2,1,0:T(8,128)(2,1)S(1)}, bf16[1,48,2304]{2,1,0:T(8,128)(2,1)}, u32[]{:S(2)}) copy-start(bf16[1,48,2304]{2,1,0:T(8,128)(2,1)} %param.15) | copy-start | bytes 663556
  0.0 1.5 %copy-start.2 = (f32[2,48,49]{2,1,0:T(8,128)S(1)}, f32[2,48,49]{2,1,0:T(8,128)}, u32[]{:S(2)}) copy-start(f32[2,48,49]{2,1,0:T(8,128)} %taps_ref.1) | copy-start | bytes 56452
  0.0 1.5 %copy-start.3 = (s32[1,2304]{1,0:T(1,128)S(1)}, s32[1,2304]{1,0:T(1,128)}, u32[]{:S(2)}) copy-start(s32[1,2304]{1,0:T(1,128)} %land_ref.1) | copy-start | bytes 27652
  0.0 1.5 %copy-start.4 = (f32[2,768]{1,0:T(2,128)S(1)}, f32[2,768]{1,0:T(2,128)}, u32[]{:S(2)}) copy-start(f32[2,768]{1,0:T(2,128)} %up_bias_ref.1) | copy-start | bytes 18436
  0.0 1.5 %copy-start.5 = (f32[2,192]{1,0:T(2,128)S(1)}, f32[2,192]{1,0:T(2,128)}, u32[]{:S(2)}) copy-start(f32[2,192]{1,0:T(2,128)} %gain_ref.1) | copy-start | bytes 4612
  0.0 1.5 %copy-start.6 = (f32[2,192]{1,0:T(2,128)S(1)}, f32[2,192]{1,0:T(2,128)}, u32[]{:S(2)}) copy-start(f32[2,192]{1,0:T(2,128)} %shift_ref.1) | copy-start | bytes 4612
  0.0 1.5 %copy-start.7 = (f32[2,192]{1,0:T(2,128)S(1)}, f32[2,192]{1,0:T(2,128)}, u32[]{:S(2)}) copy-start(f32[2,192]{1,0:T(2,128)} %down_bias_ref.1) | copy-start | bytes 4612
  0.1 1.5 %copy-start.8 = (f32[48,4]{0,1:T(4,128)S(1)}, f32[48,4]{0,1:T(4,128)}, u32[]{:S(2)}) copy-start(f32[48,4]{0,1:T(4,128)} %param.28) | copy-start | bytes 2308
  0.1 1.5 %copy-start.9 = (f32[48,4]{0,1:T(4,128)S(1)}, f32[48,4]{0,1:T(4,128)}, u32[]{:S(2)}) copy-start(f32[48,4]{0,1:T(4,128)} %param.29) | copy-start | bytes 2308
  0.1 1.5 %copy-start.10 = (f32[2,48]{1,0:T(2,128)S(1)}, f32[2,48]{1,0:T(2,128)}, u32[]{:S(2)}) copy-start(f32[2,48]{1,0:T(2,128)} %bias_ref.1) | copy-start | bytes 1156
  0.1 1.5 %copy-start.11 = (f32[2,48]{1,0:T(2,128)S(1)}, f32[2,48]{1,0:T(2,128)}, u32[]{:S(2)}) copy-start(f32[2,48]{1,0:T(2,128)} %scale_ref.1) | copy-start | bytes 1156
  0.1 1.5 %copy-start.12 = (s32[128]{0:T(128)S(1)}, s32[128]{0:T(128)}, u32[]{:S(2)}) copy-start(s32[128]{0:T(128)} %param.17) | copy-start | bytes 1540
  0.1 1.5 %copy-start.13 = (s32[128]{0:T(128)S(1)}, s32[128]{0:T(128)}, u32[]{:S(2)}) copy-start(s32[128]{0:T(128)} %param.18) | copy-start | bytes 1540
